TPU v7x, 1024 devices: a whole 4x4x32 slice. The times are simulated.
1024 devices in a mesh: slab: 16 (over y, z_hi), chan: 64 (over x, z_lo, core).
Axes of the slice: x: 4, y: 4, z: 32 (z_hi: 4, z_lo: 8; z = z_hi * 8 + z_lo), core: 2. Of those that a mesh axis runs over, the one named last changes fastest.
Arguments:
- x_in: bfloat16 [256, 32, 8, 128], P('chan', 'slab'), may hold values from -6 to 6
- weight: bfloat16 [256, 27, 256], P('chan'), may hold values from -0.21875 to 0.21875
- bias_vec: bfloat16 [256], P('chan'), may hold values from -3 to 3
- grad_out: bfloat16 [256, 32, 8, 128], P('chan', 'slab'), may hold values from -6 to 6
Outputs:
- activation: bfloat16 [256, 32, 8, 128], P('chan', 'slab')
- input_grad: bfloat16 [256, 32, 8, 128], P('chan', 'slab')
- weight_grad: float32 [256, 27, 256], P('chan')
- bias_grad: float32 [256], P('chan')
All inputs are finite; a program needn't handle non-finite values.
Results may differ from a plain program's by a relative error of at most 0.008.
Values may be sent and summed in bfloat16 or wider, within the bound.
A program may use at most 32 MiB of HBM per device.

v0:
```python
import math

import jax
import jax.numpy as jnp
from jax import lax
from jax.sharding import PartitionSpec as P


def with_halo(block, sides, width):
    for axis, dim in sides:
        count = lax.axis_size(axis)
        forward = [(i, i + 1) for i in range(count - 1)]
        forward.append((count - 1, 0))
        backward = [(target, source) for source, target in forward]
        low = lax.ppermute(
            lax.slice_in_dim(block, block.shape[dim] - width, None, axis=dim), axis, forward
        )
        high = lax.ppermute(lax.slice_in_dim(block, 0, width, axis=dim), axis, backward)
        block = jnp.concatenate([low, block, high], axis=dim)
    return block


def total_of_pieces(shard, axis):
    blocks = lax.all_gather(shard, axis)
    return blocks.sum(axis=0)


def split_up(shard, dim, count):
    shape = shard.shape
    blocks = shard.reshape(*shape[:dim], count, shape[dim] // count, *shape[dim + 1 :])
    return jnp.moveaxis(blocks, dim, 0)


def sent_and_summed(shard, axis, dim):
    count = lax.axis_size(axis)
    blocks = lax.all_to_all(split_up(shard, dim, count), axis, 0, 0, tiled=True)
    return jnp.sum(blocks, axis=0)


def tap_list():
    return [(9 * i + 3 * j + l, i, j, l) for i in range(3) for j in range(3) for l in range(3)]


def on_device(x_in, weight, bias_vec, grad_out):
    out_local, n_taps, in_total = weight.shape
    n_planes, n_rows, n_depth = (x_in.shape[1], x_in.shape[2], x_in.shape[3])
    rimmed = with_halo(x_in, (("slab", 1),), 1)
    padded = lax.all_gather(rimmed, "chan", axis=0, tiled=True)
    own_planes = padded[:, 1 : n_planes + 1]
    pre_act = (
        jnp.zeros((out_local, n_planes, n_rows, n_depth), jnp.float32)
        + bias_vec.astype(jnp.float32)[:, None, None, None]
    )
    for i in range(3):
        w_plane = jnp.transpose(weight[:, 9 * i : 9 * i + 9], (1, 0, 2)).reshape(
            9 * out_local, in_total
        )
        plane_part = jnp.dot(
            w_plane,
            padded[:, i : i + n_planes].reshape(in_total, -1),
            preferred_element_type=jnp.float32,
        )
        plane_part = plane_part.reshape(9, out_local, n_planes, n_rows, n_depth)
        for j in range(3):
            for l in range(3):
                pre_act = pre_act + jnp.roll(plane_part[3 * j + l], (1 - j, 1 - l), axis=(2, 3))
    sigmoid_v = jax.nn.sigmoid(pre_act)
    activation = (pre_act * sigmoid_v).astype(jnp.bfloat16)
    slope = sigmoid_v * (1.0 + pre_act * (1.0 - sigmoid_v))
    grad_pre = (grad_out.astype(jnp.float32) * slope).astype(jnp.bfloat16)
    padded_grad = with_halo(grad_pre, (("slab", 1),), 1)
    shifted = jnp.stack(
        [
            jnp.roll(padded_grad[:, 2 - i : 2 - i + n_planes], (j - 1, l - 1), axis=(2, 3))
            for k, i, j, l in tap_list()
        ],
        0,
    )
    shifted = shifted.reshape(n_taps * out_local, -1)
    grad_scale = 1.0 / math.sqrt(lax.axis_size("slab") * n_planes * n_rows * n_depth)
    filter_local = lax.dot_general(
        shifted,
        own_planes.reshape(in_total, -1),
        (((1,), (1,)), ((), ())),
        preferred_element_type=jnp.float32,
    )
    filter_part = (
        jnp.transpose(filter_local.reshape(n_taps, out_local, in_total), (1, 0, 2)) * grad_scale
    )
    bias_part = grad_scale * jnp.sum(grad_pre.astype(jnp.float32), axis=(1, 2, 3))
    bias_row = jnp.concatenate(
        [bias_part[:, None, None], jnp.zeros((out_local, 1, in_total - 1), jnp.float32)], 2
    )
    summed_filters = total_of_pieces(jnp.concatenate([filter_part, bias_row], 1), "slab")
    weight_grad = summed_filters[:, :n_taps]
    bias_grad = summed_filters[:, n_taps, 0]
    flat_w = jnp.transpose(weight, (1, 0, 2)).reshape(n_taps * out_local, in_total)
    product = lax.dot_general(
        flat_w, shifted, (((0,), (0,)), ((), ())), preferred_element_type=jnp.float32
    )
    grad_in = sent_and_summed(
        product.reshape(
            in_total // lax.axis_size("chan") * lax.axis_size("chan"), n_planes, n_rows, n_depth
        ),
        "chan",
        0,
    )
    return (activation, grad_in.astype(jnp.bfloat16), weight_grad, bias_grad)


def solution(mesh):
    placed = (
        P("chan", "slab", None, None),
        P("chan", None, None),
        P("chan"),
        P("chan", "slab", None, None),
    )
    return jax.shard_map(
        on_device,
        mesh=mesh,
        in_specs=placed,
        out_specs=(
            P("chan", "slab", None, None),
            P("chan", "slab", None, None),
            P("chan", None, None),
            P("chan"),
        ),
        check_vma=False,
    )
```

profile of v0, /device:TPU:1, one launch (start us, length us, event | category | flops | bytes accessed | tf_op | source)
XLA Modules:
  0.0 418.6 jit_solution(12217211871667297797)
XLA Ops:
  7.2 0.7 fusion.85
  7.9 16.2 %collective-permute-start = (bf16[4,1,8,128]{3,2,1,0:T(8,128)(2,1)S(1)}, bf16[4,1,8,128]{3,2,1,0:T(8,128)(2,1)S(1)}, u32[]{:S(2)}, u32[]{:S(2)}) collective-permute-start(bf16[4,1,8,128]{3,2,1,0:T(8,128)(2,1)S(1)} %get-tuple-element.208), channel_id=1, source_target_pairs={{0,64},{64,128},{128,192},{192,256},{256,320},{320,384},{384,448},... | collective-permute-start | bytes 24584 | tf_op jit(solution)/shard_map/ppermute | solution.py:15
  24.2 11.6 %collective-permute-start.1 = (bf16[4,1,8,128]{3,2,1,0:T(8,128)(2,1)S(1)}, bf16[4,1,8,128]{3,2,1,0:T(8,128)(2,1)S(1)}, u32[]{:S(2)}, u32[]{:S(2)}) collective-permute-start(bf16[4,1,8,128]{3,2,1,0:T(8,128)(2,1)S(1)} %get-tuple-element.209), channel_id=1, source_target_pairs={{64,0},{128,64},{192,128},{256,192},{320,256},{384,320},{448,384},... | collective-permute-start | bytes 24584 | tf_op jit(solution)/shard_map/ppermute | solution.py:18
  35.9 4.8 %collective-permute-done.1 = bf16[4,1,8,128]{3,2,1,0:T(8,128)(2,1)S(1)} collective-permute-done((bf16[4,1,8,128]{3,2,1,0:T(8,128)(2,1)S(1)}, bf16[4,1,8,128]{3,2,1,0:T(8,128)(2,1)S(1)}, u32[]{:S(2)}, u32[]{:S(2)}) %collective-permute-start.1) | collective-permute-done | bytes 8224 | tf_op jit(solution)/shard_map/ppermute | solution.py:18
  40.7 1.3 pad_maximum_fusion.16
  42.0 0.8 slice_bitcast_fusion.29
  42.8 0.6 reshape.104
  43.4 0.6 reshape.108
  44.0 1.2 convert_element_type.18
  45.2 124.5 %all-gather.4.cloned.1.call-done = bf16[256,4,8,128]{3,2,1,0:T(8,128)(2,1)} async-done(((bf16[4,4,8,128]{3,2,1,0:T(8,128)(2,1)}), bf16[256,4,8,128]{3,2,1,0:T(8,128)(2,1)}) %all-gather.4.cloned.1.call-update) | async-done | bytes 2097168 | tf_op jit(solution)/shard_map/all_gather | solution.py:48
  169.7 3.4 fusion.79
  173.0 0.8 copy.2696
  173.8 0.4 convolution_bitcast_fusion.2
  174.2 0.7 slice_bitcast_fusion.17
  175.0 1.6 copy.2731
  176.6 1.1 convolution_bitcast_fusion.3
  177.8 0.7 slice_bitcast_fusion.26
  178.5 0.8 copy.2733
  179.4 1.2 convolution_bitcast_fusion.1
  181.5 0.1 slice_maximum_fusion.7
  182.6 0.5 convert_reduce_fusion
  183.1 11.6 %collective-permute-start.2 = (bf16[4,1,8,128]{3,2,1,0:T(8,128)(2,1)S(1)}, bf16[4,1,8,128]{3,2,1,0:T(8,128)(2,1)S(1)}, u32[]{:S(2)}, u32[]{:S(2)}) collective-permute-start(bf16[4,1,8,128]{3,2,1,0:T(8,128)(2,1)S(1)} %get-tuple-element.203), channel_id=1, source_target_pairs={{64,0},{128,64},{192,128},{256,192},{320,256},{384,320},{448,384},... | collective-permute-start | bytes 24584 | tf_op jit(solution)/shard_map/ppermute | solution.py:18
  194.8 2.8 collective-permute-start.3
  197.7 12.3 %collective-permute-done.3 = bf16[4,1,8,128]{3,2,1,0:T(8,128)(2,1)S(1)} collective-permute-done((bf16[4,1,8,128]{3,2,1,0:T(8,128)(2,1)S(1)}, bf16[4,1,8,128]{3,2,1,0:T(8,128)(2,1)S(1)}, u32[]{:S(2)}, u32[]{:S(2)}) %collective-permute-start.3) | collective-permute-done | bytes 8224 | tf_op jit(solution)/shard_map/ppermute | solution.py:15
  210.2 0.1 fusion.56
  210.3 0.1 fusion.55
  210.7 0.1 fusion.66
  210.7 0.1 fusion.65
  211.4 0.1 fusion.44
  211.5 0.1 fusion.43
  213.7 1.4 stack.111
  215.1 0.2 copy.2725
  215.3 0.6 copy-done
  215.9 1.0 reshape.109
  216.9 1.5 convolution_bitcast_fusion
  218.4 1.8 copy.2726
  220.2 3.3 copy.2762
  223.5 8.8 %all-to-all-start = ((f32[64,4,2,8,128]{4,3,2,1,0:T(8,128)}), f32[64,4,2,8,128]{4,3,2,1,0:T(8,128)S(1)}, u32[]{:S(2)}, u32[]{:S(2)}) async-start(f32[64,4,2,8,128]{4,3,2,1,0:T(8,128)} %bitcast.299), calls=%async_computation | async-start | bytes 4194304 | tf_op jit(solution)/shard_map/all_to_all | solution.py:36
  232.4 0.1 copy.2727
  232.5 1.5 fusion.1
  234.0 0.7 select_maximum_fusion
  234.7 0.6 multiply_convert_fusion.1
  235.3 144.8 %all-gather.6.cloned.1.call-done = f32[64,28,256]{2,1,0:T(8,128)} async-done(((f32[4,28,256]{2,1,0:T(8,128)}), f32[64,28,256]{2,1,0:T(8,128)}) %all-gather.6.cloned.1.call-update) | async-done | bytes 1835024 | tf_op jit(solution)/shard_map/all_gather | solution.py:24
  380.1 1.8 reduce_sum.29
  381.9 0.7 copy.2728
  382.6 0.6 slice_reduce_fusion
  383.2 27.8 %all-to-all-done = f32[64,4,2,8,128]{4,3,2,1,0:T(8,128)S(1)} async-done(((f32[64,4,2,8,128]{4,3,2,1,0:T(8,128)}), f32[64,4,2,8,128]{4,3,2,1,0:T(8,128)S(1)}, u32[]{:S(2)}, u32[]{:S(2)}) %all-to-all-start) | async-done | bytes 2097184 | tf_op jit(solution)/shard_map/all_to_all | solution.py:36
  411.0 0.7 reduce_sum.27
  (146 shorter events, 4.9 us)
Async XLA Ops:
  7.2 162.5 %all-gather.4.cloned.1.call-start = ((), (), s32[]{:S(2)}) async-start(), calls=%async_computation.1 | async-start | bytes 2129920 | tf_op jit(solution)/shard_map/all_gather | solution.py:48
  7.9 27.9 %collective-permute-start = (bf16[4,1,8,128]{3,2,1,0:T(8,128)(2,1)S(1)}, bf16[4,1,8,128]{3,2,1,0:T(8,128)(2,1)S(1)}, u32[]{:S(2)}, u32[]{:S(2)}) collective-permute-start(bf16[4,1,8,128]{3,2,1,0:T(8,128)(2,1)S(1)} %get-tuple-element.208), channel_id=1, source_target_pairs={{0,64},{64,128},{128,192},{192,256},{256,320},{320,384},{384,448},... | collective-permute-start | bytes 24584 | tf_op jit(solution)/shard_map/ppermute | solution.py:15
  24.2 16.5 %collective-permute-start.1 = (bf16[4,1,8,128]{3,2,1,0:T(8,128)(2,1)S(1)}, bf16[4,1,8,128]{3,2,1,0:T(8,128)(2,1)S(1)}, u32[]{:S(2)}, u32[]{:S(2)}) collective-permute-start(bf16[4,1,8,128]{3,2,1,0:T(8,128)(2,1)S(1)} %get-tuple-element.209), channel_id=1, source_target_pairs={{64,0},{128,64},{192,128},{256,192},{320,256},{384,320},{448,384},... | collective-permute-start | bytes 24584 | tf_op jit(solution)/shard_map/ppermute | solution.py:18
  179.3 1.5 copy-start.2
  179.3 1.5 copy-start.3
  179.3 1.6 copy-start.6
  179.3 1.6 copy-start.7
  179.4 1.6 copy-start.4
  179.4 1.6 copy-start.5
  179.4 3.3 copy-start.8
  179.4 3.3 copy-start.9
  180.7 16.9 %copy-start.1 = (bf16[4,27,256]{2,0,1:T(4,128)(2,1)S(1)}, bf16[4,27,256]{2,0,1:T(4,128)(2,1)}, u32[]{:S(2)}) copy-start(bf16[4,27,256]{2,0,1:T(4,128)(2,1)} %param.5) | copy-start | bytes 165892
  183.1 14.5 %collective-permute-start.2 = (bf16[4,1,8,128]{3,2,1,0:T(8,128)(2,1)S(1)}, bf16[4,1,8,128]{3,2,1,0:T(8,128)(2,1)S(1)}, u32[]{:S(2)}, u32[]{:S(2)}) collective-permute-start(bf16[4,1,8,128]{3,2,1,0:T(8,128)(2,1)S(1)} %get-tuple-element.203), channel_id=1, source_target_pairs={{64,0},{128,64},{192,128},{256,192},{320,256},{384,320},{448,384},... | collective-permute-start | bytes 24584 | tf_op jit(solution)/shard_map/ppermute | solution.py:18
  194.8 15.2 %collective-permute-start.3 = (bf16[4,1,8,128]{3,2,1,0:T(8,128)(2,1)S(1)}, bf16[4,1,8,128]{3,2,1,0:T(8,128)(2,1)S(1)}, u32[]{:S(2)}, u32[]{:S(2)}) collective-permute-start(bf16[4,1,8,128]{3,2,1,0:T(8,128)(2,1)S(1)} %get-tuple-element.202), channel_id=1, source_target_pairs={{0,64},{64,128},{128,192},{192,256},{256,320},{320,384},{384,448},... | collective-permute-start | bytes 24584 | tf_op jit(solution)/shard_map/ppermute | solution.py:15
  215.1 0.8 copy-start
  223.5 187.5 %all-to-all-start = ((f32[64,4,2,8,128]{4,3,2,1,0:T(8,128)}), f32[64,4,2,8,128]{4,3,2,1,0:T(8,128)S(1)}, u32[]{:S(2)}, u32[]{:S(2)}) async-start(f32[64,4,2,8,128]{4,3,2,1,0:T(8,128)} %bitcast.299), calls=%async_computation | async-start | bytes 4194304 | tf_op jit(solution)/shard_map/all_to_all | solution.py:36
  232.3 147.8 %all-gather.6.cloned.1.call-start = ((), (), s32[]{:S(2)}) async-start(), calls=%async_computation.2 | async-start | bytes 2228224 | tf_op jit(solution)/shard_map/all_gather | solution.py:24
Sparse Core Ops, SparseCore 0:
  42.1 127.4 all-gather.3
  237.3 142.7 all-gather.5
where the time goes:
time: 425 us; the launch traced here: 419 us
  waiting for transfers between devices  314 us (74%)
  starting transfers between devices  51.2 us (12%)
  local copies, waits for them, and re-layouts  22.3 us (5%)
  between operations  14.9 us (4%)
  other arithmetic  10.3 us (2%)
  matrix products  5.73 us (1%)
    all_gather x1, waiting for transfers between devices, total_of_pieces(): blocks = lax.all_gather(shard, axis)  145 us
    all_gather x1, waiting for transfers between devices, on_device(): padded = lax.all_gather(rimmed, 'chan', axis=0, tiled=True)  124 us
    all_to_all x1, waiting for transfers between devices, sent_and_summed(): blocks = lax.all_to_all(split_up(shard, dim, count), axis, 0, 0, tiled=True)  27.8 us
    ppermute x2, starting transfers between devices, with_halo(): lax.ppermute(lax.slice_in_dim(block, 0, width, axis=dim), axis, backward)  23.3 us
    ppermute x2, starting transfers between devices, with_halo(): lax.ppermute(lax.slice_in_dim(block, block.shape[dim] - width, None, axis...  19.1 us
    ppermute x2, waiting for transfers between devices, with_halo(): lax.ppermute(lax.slice_in_dim(block, block.shape[dim] - width, None, axis...  12.3 us
    all_to_all x1, starting transfers between devices, sent_and_summed(): blocks = lax.all_to_all(split_up(shard, dim, count), axis, 0, 0, tiled=True)  8.78 us
    unnamed x27, local copies, waits for them, and re-layouts  8.54 us
  transfers between devices with their start and end apart: 7, of which 5 were waited for; matrix products, arithmetic and copies ran while one was open for 2% of the time, Pallas kernels for 0%

commit v1 on v0

v1 whole, which is shorter than its diff:
```python
import functools
import math

import jax
import jax.numpy as jnp
from jax import lax
from jax.experimental import pallas as pl
from jax.experimental.pallas import tpu as pltpu
from jax.sharding import PartitionSpec as P

MESH = pl.DeviceIdType.MESH
F32, BF16 = jnp.float32, jnp.bfloat16
NX, NZ, NK = 4, 8, 2
NY, NH = 4, 4
NT = (((1,), (1,)), ((), ()))


class Copies:
    def __init__(self, send_sems):
        self.send_sems = send_sems
        self.started = []

    def send(self, src, dst, recv_sem, device):
        copy = pltpu.make_async_remote_copy(
            src_ref=src,
            dst_ref=dst,
            send_sem=self.send_sems.at[len(self.started)],
            recv_sem=recv_sem,
            device_id=device,
            device_id_type=MESH,
        )
        copy.start()
        self.started.append(copy)

    def drain(self):
        for copy in self.started:
            copy.wait_send()


def landed(dst, recv_sem):
    here = (lax.axis_index("slab"), lax.axis_index("chan"))
    pltpu.make_async_remote_copy(
        src_ref=dst, dst_ref=dst, send_sem=recv_sem, recv_sem=recv_sem, device_id=here, device_id_type=MESH
    ).wait_recv()


class Gather:
    def __init__(self, copies, place, buf, rz, rx, rc, rh):
        self.c = copies
        self.slab, self.x, self.z, self.k = place
        self.h, self.z4 = self.z // 4, self.z % 4
        self.mates = [(self.z4 + m) % 4 for m in range(1, 4)]
        self.buf, self.rz, self.rx, self.rc, self.rh = buf, rz, rx, rc, rh

    def dev(self, x, z, k):
        return (self.slab, (x * NZ + z) * NK + k)

    def borders(self):
        me = (self.x * NZ + self.z) * NK + self.k
        after, before = (self.slab + 1) % (NY * NH), (self.slab + NY * NH - 1) % (NY * NH)
        own = lambda q, p: self.buf.at[q, p, self.x, self.h, self.z4, self.k]
        self.c.send(own(0, 1), own(1, 0), self.rh.at[0], (after, me))
        self.c.send(own(0, 0), own(1, 1), self.rh.at[1], (before, me))

    def wait_borders(self):
        for side in range(2):
            landed(self.buf.at[1, side, self.x, self.h, self.z4, self.k], self.rh.at[side])

    def block(self, q, h, z4):
        return self.buf.at[q, :, self.x, h, z4, self.k]

    def piece(self, q, x, h, k):
        return self.buf.at[q, :, x, h, :, k]

    def z_send(self, q):
        mine = self.block(q, self.h, self.z4)
        for mate in self.mates:
            self.c.send(mine, mine, self.rz.at[q, self.z], self.dev(self.x, self.h * 4 + mate, self.k))
        self.c.send(mine, mine, self.rz.at[q, self.z], self.dev(self.x, (1 - self.h) * 4 + self.z4, self.k))

    def z_mates(self, q):
        for mate in self.mates:
            landed(self.block(q, self.h, mate), self.rz.at[q, self.h * 4 + mate])

    def z_mirror(self, q):
        other = (1 - self.h) * 4 + self.z4
        theirs = self.block(q, 1 - self.h, self.z4)
        landed(theirs, self.rz.at[q, other])
        for mate in self.mates:
            self.c.send(theirs, theirs, self.rz.at[q, other], self.dev(self.x, self.h * 4 + mate, self.k))

    def z_far(self, q):
        for mate in self.mates:
            landed(self.block(q, 1 - self.h, mate), self.rz.at[q, (1 - self.h) * 4 + mate])

    def c_send(self, q, x, h):
        mine = self.piece(q, x, h, self.k)
        self.c.send(mine, mine, self.rc.at[q, h, x], self.dev(self.x, self.z, 1 - self.k))

    def x_send(self, q, h):
        mine = self.piece(q, self.x, h, self.k)
        for step in (1, 3):
            self.c.send(mine, mine, self.rx.at[q, h, self.x], self.dev((self.x + step) % 4, self.z, self.k))
        self.c_send(q, self.x, h)

    def x_near(self, q, h):
        for step in (1, 3):
            x = (self.x + step) % 4
            landed(self.piece(q, x, h, self.k), self.rx.at[q, h, x])
        source, target = (self.x + 3 + 2 * self.k) % 4, (self.x + 1 + 2 * self.k) % 4
        passed = self.piece(q, source, h, self.k)
        self.c.send(passed, passed, self.rx.at[q, h, source], self.dev(target, self.z, self.k))
        for step in (1, 3):
            self.c_send(q, (self.x + step) % 4, h)

    def x_far(self, q, h):
        x = (self.x + 2) % 4
        landed(self.piece(q, x, h, self.k), self.rx.at[q, h, x])
        self.c_send(q, x, h)

    def c_wait(self, q):
        for h in range(2):
            for x in range(4):
                landed(self.piece(q, x, h, 1 - self.k), self.rc.at[q, h, x])

    def plane(self, q, p):
        return self.buf[q, p].reshape(2048, 128)

    def pair(self, q):
        return jnp.concatenate([self.plane(q, 0), self.plane(q, 1)], axis=1)


def band_weights(expanded, out, row_of, sign):
    lane = lax.broadcasted_iota(jnp.int32, (8, 2048), 1)
    sub = lax.broadcasted_iota(jnp.int32, (8, 2048), 0)
    tap = (sign * (lane - sub) + 1) & 7

    def one(t):
        rows = [expanded[pl.ds(row_of(t, j), 1), :] for j in range(3)]
        return jnp.where(tap == 0, rows[0], jnp.where(tap == 1, rows[1], jnp.where(tap == 2, rows[2], 0.0)))

    def body(u, carry):
        both = jnp.concatenate([one(2 * u), one(2 * u + 1)], axis=0)
        out[pl.ds(pl.multiple_of(16 * u, 16), 16), :] = both.astype(BF16)
        return carry

    lax.fori_loop(0, 18, body, 0)


def kernel(
    scale,
    x_ref, w1_ref, w2_ref, bias_ref, go_ref,
    act_ref, ig_ref, wg_ref, bg_ref,
    xb, gb, rep, wide, wa, wb, dm, dw, yb, zb, tot,
    send_sems, xz, xx, xc, xh, gz, gx, gc, gh, sy, sz, sg,
):
    slab, chan = lax.axis_index("slab"), lax.axis_index("chan")
    y, zh = slab // NH, slab % NH
    x, z, k = chan // (NZ * NK), chan // NK % NZ, chan % NK
    place = (slab, x, z, k)
    copies = Copies(send_sems)
    gx_ = Gather(copies, place, xb, xz, xx, xc, xh)
    gg_ = Gather(copies, place, gb, gz, gx, gc, gh)
    h, f = gx_.h, 1 - gx_.h
    at = lambda yy, hh: (yy * NH + hh, chan)

    partners = [gx_.dev(x, z, 1 - k)]
    partners += [gx_.dev((x + s) % 4, z, k) for s in (1, 3)]
    partners += [gx_.dev(x, h * 4 + m, k) for m in gx_.mates] + [gx_.dev(x, f * 4 + gx_.z4, k)]
    partners += [at((y + m) % NY, zh) for m in range(1, NY)]
    partners += [at(y, (zh + s) % NH) for s in (1, NH - 1)]
    partners += [((slab + s) % (NY * NH), chan) for s in (1, NY * NH - 1)]
    barrier = pltpu.get_barrier_semaphore()
    for partner in partners:
        pl.semaphore_signal(barrier, inc=1, device_id=partner, device_id_type=MESH)

    for p in range(2):
        xb[0, p, x, h, gx_.z4, k] = x_ref[p]
    for n in range(8):
        row = lax.broadcasted_iota(jnp.int32, (256, 256), 0)
        col = lax.broadcasted_iota(jnp.int32, (256, 256), 1)
        rep[:, 256 * n : 256 * n + 256] = jnp.where(row == 32 * n + (col >> 3), 1.0, 0.0).astype(BF16)

    pl.semaphore_wait(barrier, len(partners))
    gx_.borders()
    gx_.z_send(0)

    for n in range(8):
        wide[0:108, 256 * n : 256 * n + 256] = jnp.dot(
            w1_ref[...], rep[:, 256 * n : 256 * n + 256], preferred_element_type=F32
        )
    band_weights(wide, wa, lambda t, j: t // 12 * 36 + j * 12 + t % 12, 1)

    gx_.z_mates(0)
    gx_.x_send(0, h)
    gx_.z_mirror(0)
    gx_.x_near(0, h)
    gx_.wait_borders()
    gx_.z_send(1)
    gx_.z_far(0)
    gx_.x_send(0, f)
    gx_.x_far(0, h)
    gx_.z_mates(1)
    gx_.x_send(1, h)
    gx_.z_mirror(1)
    gx_.x_near(0, f)
    gx_.x_far(0, f)
    gx_.x_near(1, h)
    gx_.z_far(1)
    gx_.x_send(1, f)
    gx_.x_far(1, h)

    for c in range(4):
        turned = w2_ref[c].astype(F32).T.astype(BF16)
        for n in range(8):
            total = jnp.zeros((32, 256), F32)
            for o in range(4):
                row = lax.broadcasted_iota(jnp.int32, (64, 256), 0)
                col = lax.broadcasted_iota(jnp.int32, (64, 256), 1)
                pick = jnp.where(row * 4 + o == 32 * n + (col >> 3), 1.0, 0.0).astype(BF16)
                total += jnp.dot(turned[32 * o : 32 * o + 32], pick, preferred_element_type=F32)
            wide[32 * c : 32 * c + 32, 256 * n : 256 * n + 256] = total
    band_weights(wide, wb, lambda t, j: t % 4 * 32 + t // 12 * 9 + j * 3 + t % 12 // 4, -1)

    gx_.x_near(1, f)
    gx_.x_far(1, f)
    gx_.c_wait(0)
    gx_.c_wait(1)

    own = jnp.dot(wa[...], gx_.pair(0), preferred_element_type=F32)
    rim = jnp.dot(wa[...], gx_.pair(1), preferred_element_type=F32)

    def part(value, i, l, o, p):
        base = ((i * 3 + l) * 4 + o) * 8
        return value[base : base + 8, 128 * p : 128 * p + 128]

    grads = []
    for p in range(2):
        row = []
        for o in range(4):
            pre = jnp.full((8, 128), bias_ref[o], F32)
            for l in range(3):
                if p == 0:
                    term = part(rim, 0, l, o, 0) + part(own, 1, l, o, 0) + part(own, 2, l, o, 1)
                else:
                    term = part(own, 0, l, o, 0) + part(own, 1, l, o, 1) + part(rim, 2, l, o, 1)
                pre += term if l == 1 else pltpu.roll(term, (1 - l) % 128, 1)
            sig = 1.0 / (1.0 + jnp.exp(-pre))
            act_ref[o, p] = (pre * sig).astype(BF16)
            row.append(go_ref[o, p].astype(F32) * (sig * (1.0 + pre * (1.0 - sig))))
        grads.append(jnp.concatenate(row, axis=0).astype(BF16))
        gb[0, p, x, h, gx_.z4, k] = grads[p]

    gg_.borders()
    gg_.z_send(0)

    plain = jnp.concatenate(grads, axis=1).astype(F32)
    left, right = plain[:, :128], plain[:, 128:]
    turns = []
    for l in range(3):
        both = plain
        if l != 1:
            both = jnp.concatenate([pltpu.roll(v, (l - 1) % 128, 1) for v in (left, right)], axis=1)
        turns.append(both)
    rolled = jnp.concatenate(turns, axis=0).astype(BF16)
    lane = lax.broadcasted_iota(jnp.int32, (8, 2048), 1)
    sub = lax.broadcasted_iota(jnp.int32, (8, 2048), 0)
    tap = (lane - sub + 1) & 7
    planes = ((1, 0), (0, 0), (0, 1), (1, 1))
    sums = []
    for i in range(3):
        right_side = jnp.concatenate([gx_.plane(*planes[i]), gx_.plane(*planes[i + 1])], axis=1)
        full = lax.dot_general(rolled, right_side, NT, preferred_element_type=F32).reshape(12, 8, 2048)
        for j in range(3):
            kept = jnp.where((tap == j)[None], full, 0.0)
            dm[96 * j : 96 * j + 96, :] = kept.reshape(96, 2048).astype(BF16)
        folded = lax.dot_general(dm[...], rep[...], NT, preferred_element_type=F32)
        sums.append(jnp.sum(folded.reshape(36, 8, 256), axis=1))
    per_o = jnp.sum(plain.reshape(4, 8, 256), axis=(1, 2), keepdims=True).reshape(4, 1)
    sums.append(jnp.broadcast_to(per_o, (4, 256)))
    sums.append(jnp.zeros((16, 256), F32))
    dw[...] = jnp.concatenate(sums, axis=0).reshape(4, 32, 256)
    for m in range(1, NY):
        copies.send(dw.at[(y + m) % NY], yb.at[y], sy.at[y], at((y + m) % NY, zh))

    gg_.z_mates(0)
    gg_.x_send(0, h)
    gg_.z_mirror(0)
    yb[y] = dw[y]
    for m in range(1, NY):
        landed(yb.at[(y + m) % NY], sy.at[(y + m) % NY])
    zb[zh] = (yb[0] + yb[1] + yb[2] + yb[3]).astype(BF16)
    for s in (1, NH - 1):
        copies.send(zb.at[zh], zb.at[zh], sz.at[zh], at(y, (zh + s) % NH))

    gg_.x_near(0, h)
    gg_.wait_borders()
    gg_.z_send(1)
    gg_.z_far(0)
    gg_.x_send(0, f)
    gg_.x_far(0, h)
    gg_.z_mates(1)
    gg_.x_send(1, h)
    gg_.z_mirror(1)
    gg_.x_near(0, f)
    for s in (1, NH - 1):
        landed(zb.at[(zh + s) % NH], sz.at[(zh + s) % NH])
    source, target = (zh + 3 + 2 * k) % NH, (zh + 1 + 2 * k) % NH
    copies.send(zb.at[source], zb.at[source], sz.at[source], at(y, target))
    gg_.x_far(0, f)
    gg_.x_near(1, h)
    gg_.z_far(1)
    gg_.x_send(1, f)
    gg_.x_far(1, h)
    gg_.x_near(1, f)
    gg_.c_wait(0)
    own2 = jnp.dot(wb[...], gg_.pair(0), preferred_element_type=F32)
    landed(zb.at[(zh + 2) % NH], sz.at[(zh + 2) % NH])
    total = zb[0].astype(F32) + zb[1].astype(F32) + zb[2].astype(F32) + zb[3].astype(F32)
    tot[y] = total * scale
    for m in range(1, NY):
        copies.send(tot.at[y], tot.at[y], sg.at[y], at((y + m) % NY, zh))
    gg_.x_far(1, f)
    gg_.c_wait(1)
    rim2 = jnp.dot(wb[...], gg_.pair(1), preferred_element_type=F32)
    for p in range(2):
        for c in range(4):
            out = jnp.zeros((8, 128), F32)
            for l in range(3):
                if p == 0:
                    term = part(own2, 0, l, c, 1) + part(own2, 1, l, c, 0) + part(rim2, 2, l, c, 0)
                else:
                    term = part(rim2, 0, l, c, 1) + part(own2, 1, l, c, 1) + part(own2, 2, l, c, 0)
                out += term if l == 1 else pltpu.roll(term, (l - 1) % 128, 1)
            ig_ref[c, p] = out.astype(BF16)
    for m in range(1, NY):
        landed(tot.at[(y + m) % NY], sg.at[(y + m) % NY])
    everything = tot[...].reshape(128, 256)
    for t in range(27):
        wg_ref[t] = everything[4 * t : 4 * t + 4]
    bg_ref[...] = everything[108:112, :128]
    copies.drain()


def on_device(x_in, weight, bias_vec, grad_out):
    n_cells = lax.axis_size("slab") * x_in.shape[1] * x_in.shape[2] * x_in.shape[3]
    scale = 1.0 / math.sqrt(n_cells)
    planes = jnp.transpose(x_in, (1, 0, 2, 3)).reshape(2, 32, 128)
    by_tap = jnp.transpose(weight, (1, 0, 2)).reshape(108, 256)
    turned = jnp.pad(weight, ((0, 0), (0, 5), (0, 0))).reshape(128, 256).T.reshape(64, 4, 128)
    turned = lax.all_to_all(turned, "chan", 0, 0, tiled=True)
    turned = jnp.transpose(turned, (1, 0, 2))
    dma = lambda *shape: pltpu.SemaphoreType.DMA(shape)
    gathered = pltpu.VMEM((2, 2, NX, 2, 4, NK, 32, 128), BF16)
    vmem = pl.BlockSpec(memory_space=pltpu.VMEM)
    act, grad_in, filters, bias_grad = pl.pallas_call(
        functools.partial(kernel, scale),
        out_shape=(
            jax.ShapeDtypeStruct((4, 2, 8, 128), BF16),
            jax.ShapeDtypeStruct((4, 2, 8, 128), BF16),
            jax.ShapeDtypeStruct((27, 4, 256), F32),
            jax.ShapeDtypeStruct((4, 128), F32),
        ),
        in_specs=[vmem, vmem, vmem, pl.BlockSpec(memory_space=pltpu.SMEM), vmem],
        out_specs=(vmem,) * 4,
        scratch_shapes=[
            gathered,
            gathered,
            pltpu.VMEM((256, 2048), BF16),
            pltpu.VMEM((128, 2048), F32),
            pltpu.VMEM((288, 2048), BF16),
            pltpu.VMEM((288, 2048), BF16),
            pltpu.VMEM((288, 2048), BF16),
            pltpu.VMEM((4, 32, 256), F32),
            pltpu.VMEM((4, 32, 256), F32),
            pltpu.VMEM((4, 32, 256), BF16),
            pltpu.VMEM((4, 32, 256), F32),
            dma(100),
            *([dma(2, 8), dma(2, 2, 4), dma(2, 2, 4), dma(2)] * 2),
            dma(4),
            dma(4),
            dma(4),
        ],
        compiler_params=pltpu.CompilerParams(collective_id=0, has_side_effects=True),
    )(planes, by_tap, turned, bias_vec.astype(F32), grad_out)
    return (act, grad_in, jnp.transpose(filters, (1, 0, 2)), bias_grad[:, 0])


def solution(mesh):
    placed = (
        P("chan", "slab", None, None),
        P("chan", None, None),
        P("chan"),
        P("chan", "slab", None, None),
    )
    return jax.shard_map(
        on_device,
        mesh=mesh,
        in_specs=placed,
        out_specs=(
            P("chan", "slab", None, None),
            P("chan", "slab", None, None),
            P("chan", None, None),
            P("chan"),
        ),
        check_vma=False,
    )
```

time: 425 us -> 116 us (0.27); the launches traced: 419 us -> 116 us
  waiting for transfers between devices: 314 us -> 11.1 us
  Pallas kernels: 0 us -> 76.8 us
  starting transfers between devices: 51.2 us -> 18.3 us
  between operations: 14.9 us -> 0.69 us
  local copies, waits for them, and re-layouts: 22.3 us -> 8.26 us
  other arithmetic: 10.3 us -> 0.51 us
  matrix products: 5.73 us -> 0 us
    all_gather x2 -> x0, waiting for transfers between devices: 269 us -> none  [the longest x1 145 us: total_of_pieces(): blocks = lax.all_gather(shard, axis)]
    pallas_call x0 -> x1, Pallas kernels: none -> 76.8 us  [on_device(): pl.pallas_call(functools.partial(kernel, scale), out_shape=(jax.ShapeDtyp...]
    ppermute x4 -> x0, starting transfers between devices: 42.3 us -> none  [the longest x2 23.3 us: with_halo(): lax.ppermute(lax.slice_in_dim(block, 0, width, axis=dim), axis, backward)]
    ppermute x4 -> x0, waiting for transfers between devices: 17.1 us -> none  [the longest x2 12.3 us: with_halo(): lax.ppermute(lax.slice_in_dim(block, block.shape[dim] - width, None, axis...]
    all_to_all x1, waiting for transfers between devices: 27.8 us -> 11.1 us  [on_device(): turned = lax.all_to_all(turned, 'chan', 0, 0, tiled=True)]
    all_to_all x1, starting transfers between devices: 8.78 us -> 18.3 us  [on_device(): turned = lax.all_to_all(turned, 'chan', 0, 0, tiled=True)]
    slice x42 -> x1, local copies, waits for them, and re-layouts: 6.39 us -> 0.63 us  [on_device(): return (act, grad_in, jnp.transpose(filters, (1, 0, 2)), bias_grad[:, 0])]
    dot_general x5 -> x0, matrix products: 5.73 us -> none  [the longest x3 2.71 us: on_device(): jnp.dot(w_plane, padded[:, i:i + n_planes].reshape(in_total, -1), preferr...]
  transfers between devices with their start and end apart: 7 -> 1, of which waited for: 5 -> 1; matrix products, arithmetic and copies ran while one was open for 2% -> 2% of each run, Pallas kernels for 0% -> 0%
where the time goes in v1:
time: 116 us
  Pallas kernels  76.8 us (66%)
  starting transfers between devices  18.3 us (16%)
  waiting for transfers between devices  11.1 us (10%)
  local copies, waits for them, and re-layouts  8.26 us (7%)
    pallas_call x1, Pallas kernels, on_device(): pl.pallas_call(functools.partial(kernel, scale), out_shape=(jax.ShapeDtyp...  76.8 us
    all_to_all x1, starting transfers between devices, on_device(): turned = lax.all_to_all(turned, 'chan', 0, 0, tiled=True)  18.3 us
    all_to_all x1, waiting for transfers between devices, on_device(): turned = lax.all_to_all(turned, 'chan', 0, 0, tiled=True)  11.1 us
    unnamed x14, local copies, waits for them, and re-layouts  5.01 us
  transfers between devices with their start and end apart: 1, of which 1 were waited for; matrix products, arithmetic and copies ran while one was open for 2% of the time, Pallas kernels for 0%

profile of v1, /device:TPU:1, one launch (start us, length us, event | category | flops | bytes accessed | tf_op | source)
XLA Modules:
  0.0 115.7 jit_solution(13763954841670604355)
XLA Ops:
  0.6 0.0 copy-start
  0.6 0.8 copy.14
  1.5 0.7 copy.15
  2.2 0.0 copy-start.4
  2.2 0.0 copy-start.1
  2.2 18.3 %all-to-all-start = ((bf16[64,4,128]{2,1,0:T(4,128)(2,1)}), bf16[64,4,128]{2,1,0:T(4,128)(2,1)S(1)}, u32[]{:S(2)}, u32[]{:S(2)}) async-start(bf16[64,4,128]{2,1,0:T(4,128)(2,1)} %bitcast.5), calls=%async_computation | async-start | bytes 131072 | tf_op jit(solution)/shard_map/all_to_all | solution.py:351
  20.5 0.0 copy-done.4
  20.5 0.5 convert_element_type.5.bias_ref
  21.1 0.0 copy-done.1
  21.1 0.6 reshape.21.w1_ref
  21.7 0.0 copy-done
  21.7 0.6 copy_bitcast_fusion.1.x_ref
  22.3 11.1 %all-to-all-done = bf16[64,4,128]{2,1,0:T(4,128)(2,1)S(1)} async-done(((bf16[64,4,128]{2,1,0:T(4,128)(2,1)}), bf16[64,4,128]{2,1,0:T(4,128)(2,1)S(1)}, u32[]{:S(2)}, u32[]{:S(2)}) %all-to-all-start) | async-done | bytes 65568 | tf_op jit(solution)/shard_map/all_to_all | solution.py:351
  33.5 0.6 copy.19
  34.1 76.8 %shard_map.75 = (bf16[4,2,8,128]{3,2,1,0:T(8,128)(2,1)}, bf16[4,2,8,128]{3,2,1,0:T(8,128)(2,1)}, f32[27,4,256]{2,1,0:T(4,128)}, f32[4,128]{1,0:T(4,128)}) custom-call(bf16[2,32,128]{2,1,0:T(8,128)(2,1)} %copy_bitcast_fusion.1.x_ref, bf16[108,256]{1,0:T(8,128)(2,1)} %reshape.21.w1_ref, bf16[4,64,128]{2,1,0:T(8,128)(2,1)} %bitcast.14, ...), custom_call_target="tpu_custom_call" | custom-call | tf_op jit(solution)/shard_map/pallas_call | solution.py:356
  110.9 0.0 copy-start.3
  110.9 0.7 copy-done.3
  111.6 0.6 slice_reduce_fusion
  112.2 0.0 copy-start.2
  112.2 1.3 %copy.23 = bf16[4,2,8,128]{3,2,1,0:T(8,128)(2,1)} copy(bf16[4,2,8,128]{3,2,1,0:T(8,128)(2,1)} %get-tuple-element.16) | data formatting | bytes 32768
  113.6 0.0 copy-done.2
  113.6 0.6 copy.24
  114.2 1.5 %copy.25 = f32[4,27,256]{2,0,1:T(4,128)} copy(f32[4,27,256]{2,0,1:T(4,128)} %bitcast.17) | data formatting | bytes 221184
  (1 shorter events, 0.0 us)
Async XLA Ops:
  0.6 21.1 %copy-start = (bf16[4,2,8,128]{3,2,1,0:T(8,128)(2,1)S(1)}, bf16[4,2,8,128]{3,2,1,0:T(8,128)(2,1)}, u32[]{:S(2)}) copy-start(bf16[4,2,8,128]{3,2,1,0:T(8,128)(2,1)} %param.4) | copy-start | bytes 49156
  2.2 18.3 %copy-start.4 = (bf16[4]{0:T(256)(128)(2,1)S(1)}, bf16[4]{0:T(256)(128)(2,1)}, u32[]{:S(2)}) copy-start(bf16[4]{0:T(256)(128)(2,1)} %param.6) | copy-start | bytes 28
  2.2 18.8 %copy-start.1 = (bf16[4,27,256]{2,0,1:T(4,128)(2,1)S(1)}, bf16[4,27,256]{2,0,1:T(4,128)(2,1)}, u32[]{:S(2)}) copy-start(bf16[4,27,256]{2,0,1:T(4,128)(2,1)} %param.5) | copy-start | bytes 165892
  2.2 31.2 %all-to-all-start = ((bf16[64,4,128]{2,1,0:T(4,128)(2,1)}), bf16[64,4,128]{2,1,0:T(4,128)(2,1)S(1)}, u32[]{:S(2)}, u32[]{:S(2)}) async-start(bf16[64,4,128]{2,1,0:T(4,128)(2,1)} %bitcast.5), calls=%async_computation | async-start | bytes 131072 | tf_op jit(solution)/shard_map/all_to_all | solution.py:351
  110.9 0.7 copy-start.3
  112.2 1.3 %copy-start.2 = (bf16[4,2,8,128]{3,2,1,0:T(8,128)(2,1)S(1)}, bf16[4,2,8,128]{3,2,1,0:T(8,128)(2,1)}, u32[]{:S(2)}) copy-start(bf16[4,2,8,128]{3,2,1,0:T(8,128)(2,1)} %get-tuple-element.17) | copy-start | bytes 49156

commit v2 on v1

--- a/solution.py
+++ b/solution.py
@@ -147,12 +147,31 @@
     lax.fori_loop(0, 18, body, 0)
 
 
+def turned_weights(all_rows, spread, wide, k):
+    row = lax.broadcasted_iota(jnp.int32, (64, 256), 0)
+    col = lax.broadcasted_iota(jnp.int32, (64, 256), 1)
+    source = jnp.where(row < 32, 2 * row + k, 2 * row - 63 - k)
+    within = lax.broadcasted_iota(jnp.int32, (27, 128), 1) // 8 % 4
+    for c in range(4):
+        low, high = [all_rows[pl.ds(4 * q + c, 64, stride=8), :] for q in range(2)]
+        mine = jnp.where(k == 0, low, high).T.astype(BF16)
+        for n in range(8):
+            pick = jnp.where(source == 8 * n + (col >> 5), 1.0, 0.0).astype(BF16)
+            full = jnp.dot(mine, pick, preferred_element_type=F32)
+            for half in range(2):
+                spread[2 * n + half] = full[:, 128 * half : 128 * half + 128]
+                total = spread[2 * n + half, pl.ds(0, 27, stride=4), :]
+                for o in range(1, 4):
+                    total = jnp.where(within == o, spread[2 * n + half, pl.ds(o, 27, stride=4), :], total)
+                wide[32 * c : 32 * c + 27, 256 * n + 128 * half : 256 * n + 128 * half + 128] = total
+
+
 def kernel(
     scale,
-    x_ref, w1_ref, w2_ref, bias_ref, go_ref,
-    act_ref, ig_ref, wg_ref, bg_ref,
-    xb, gb, rep, wide, wa, wb, dm, dw, yb, zb, tot,
-    send_sems, xz, xx, xc, xh, gz, gx, gc, gh, sy, sz, sg,
+    x_ref, w_ref, bias_ref, go_ref,
+    act_ref, ig_ref, out_ref,
+    xb, gb, rep, wide, spread, wa, wb, dm, rows, t1, t2, t3, t4, all_rows, dw, yb, zb, tot, po, pi,
+    send_sems, xz, xx, xc, xh, gz, gx, gc, s1, s2, s3, sy, sz, sg, sp,
 ):
     slab, chan = lax.axis_index("slab"), lax.axis_index("chan")
     y, zh = slab // NH, slab % NH
@@ -160,68 +179,73 @@
     place = (slab, x, z, k)
     copies = Copies(send_sems)
     gx_ = Gather(copies, place, xb, xz, xx, xc, xh)
-    gg_ = Gather(copies, place, gb, gz, gx, gc, gh)
+    gg_ = Gather(copies, place, gb, gz, gx, gc, None)
     h, f = gx_.h, 1 - gx_.h
     at = lambda yy, hh: (yy * NH + hh, chan)
+    line = [(z + m) % NZ for m in range(1, NZ)]
+    ring = [(x + m) % NX for m in range(1, NX)]
+    after, before = ((slab + 1) % (NY * NH), chan), ((slab + NY * NH - 1) % (NY * NH), chan)
 
     partners = [gx_.dev(x, z, 1 - k)]
-    partners += [gx_.dev((x + s) % 4, z, k) for s in (1, 3)]
-    partners += [gx_.dev(x, h * 4 + m, k) for m in gx_.mates] + [gx_.dev(x, f * 4 + gx_.z4, k)]
+    partners += [gx_.dev(xx_, z, k) for xx_ in ring]
+    partners += [gx_.dev(x, zz, k) for zz in line]
     partners += [at((y + m) % NY, zh) for m in range(1, NY)]
     partners += [at(y, (zh + s) % NH) for s in (1, NH - 1)]
-    partners += [((slab + s) % (NY * NH), chan) for s in (1, NY * NH - 1)]
+    partners += [after, before]
     barrier = pltpu.get_barrier_semaphore()
     for partner in partners:
         pl.semaphore_signal(barrier, inc=1, device_id=partner, device_id_type=MESH)
 
     for p in range(2):
-        xb[0, p, x, h, gx_.z4, k] = x_ref[p]
+        xb[0, p, x, h, gx_.z4, k] = x_ref[:, p].astype(F32).reshape(32, 128).astype(BF16)
+    rows[104:128, :] = jnp.zeros((24, 256), F32)
+    for t in range(27):
+        rows[4 * t : 4 * t + 4, :] = w_ref[t].astype(F32)
+    t1[...] = rows[...].T.reshape(4, 8, 8, 128).astype(BF16)
     for n in range(8):
         row = lax.broadcasted_iota(jnp.int32, (256, 256), 0)
         col = lax.broadcasted_iota(jnp.int32, (256, 256), 1)
         rep[:, 256 * n : 256 * n + 256] = jnp.where(row == 32 * n + (col >> 3), 1.0, 0.0).astype(BF16)
+    by_tap = rows[...].astype(BF16)
+    for n in range(8):
+        wide[:, 256 * n : 256 * n + 256] = jnp.dot(
+            by_tap, rep[:, 256 * n : 256 * n + 256], preferred_element_type=F32
+        )
+    band_weights(wide, wa, lambda t, j: t // 12 * 36 + j * 12 + t % 12, 1)
 
     pl.semaphore_wait(barrier, len(partners))
     gx_.borders()
     gx_.z_send(0)
-
-    for n in range(8):
-        wide[0:108, 256 * n : 256 * n + 256] = jnp.dot(
-            w1_ref[...], rep[:, 256 * n : 256 * n + 256], preferred_element_type=F32
-        )
-    band_weights(wide, wa, lambda t, j: t // 12 * 36 + j * 12 + t % 12, 1)
+    for zz in line:
+        copies.send(t1.at[:, zz], t2.at[z], s1.at[z], gx_.dev(x, zz, k))
+    t2[z] = t1[:, z]
 
     gx_.z_mates(0)
     gx_.x_send(0, h)
     gx_.z_mirror(0)
     gx_.x_near(0, h)
+    gx_.z_far(0)
+    gx_.x_send(0, f)
     gx_.wait_borders()
     gx_.z_send(1)
-    gx_.z_far(0)
-    gx_.x_send(0, f)
     gx_.x_far(0, h)
+    for zz in line:
+        landed(t2.at[zz], s1.at[zz])
+    for xx_ in ring:
+        copies.send(t2.at[:, xx_], t3.at[x], s2.at[x], gx_.dev(xx_, z, k))
+    t3[x] = t2[:, x]
     gx_.z_mates(1)
     gx_.x_send(1, h)
     gx_.z_mirror(1)
     gx_.x_near(0, f)
+    gx_.x_near(1, h)
     gx_.x_far(0, f)
-    gx_.x_near(1, h)
     gx_.z_far(1)
     gx_.x_send(1, f)
     gx_.x_far(1, h)
-
-    for c in range(4):
-        turned = w2_ref[c].astype(F32).T.astype(BF16)
-        for n in range(8):
-            total = jnp.zeros((32, 256), F32)
-            for o in range(4):
-                row = lax.broadcasted_iota(jnp.int32, (64, 256), 0)
-                col = lax.broadcasted_iota(jnp.int32, (64, 256), 1)
-                pick = jnp.where(row * 4 + o == 32 * n + (col >> 3), 1.0, 0.0).astype(BF16)
-                total += jnp.dot(turned[32 * o : 32 * o + 32], pick, preferred_element_type=F32)
-            wide[32 * c : 32 * c + 32, 256 * n : 256 * n + 256] = total
-    band_weights(wide, wb, lambda t, j: t % 4 * 32 + t // 12 * 9 + j * 3 + t % 12 // 4, -1)
-
+    for xx_ in ring:
+        landed(t3.at[xx_], s2.at[xx_])
+    copies.send(t3, t4, s3, gx_.dev(x, z, 1 - k))
     gx_.x_near(1, f)
     gx_.x_far(1, f)
     gx_.c_wait(0)
@@ -234,24 +258,30 @@
         base = ((i * 3 + l) * 4 + o) * 8
         return value[base : base + 8, 128 * p : 128 * p + 128]
 
+    def turned_sum(terms, sign):
+        total = None
+        for l in range(3):
+            term = terms(l)
+            term = term if l == 1 else pltpu.roll(term, sign * (1 - l) % 128, 1)
+            total = term if total is None else total + term
+        return total
+
+    offsets = bias_ref[...].astype(F32)
     grads = []
     for p in range(2):
         row = []
         for o in range(4):
-            pre = jnp.full((8, 128), bias_ref[o], F32)
-            for l in range(3):
-                if p == 0:
-                    term = part(rim, 0, l, o, 0) + part(own, 1, l, o, 0) + part(own, 2, l, o, 1)
-                else:
-                    term = part(own, 0, l, o, 0) + part(own, 1, l, o, 1) + part(rim, 2, l, o, 1)
-                pre += term if l == 1 else pltpu.roll(term, (1 - l) % 128, 1)
+            if p == 0:
+                terms = lambda l: part(rim, 0, l, o, 0) + part(own, 1, l, o, 0) + part(own, 2, l, o, 1)
+            else:
+                terms = lambda l: part(own, 0, l, o, 0) + part(own, 1, l, o, 1) + part(rim, 2, l, o, 1)
+            pre = turned_sum(terms, 1) + offsets[:, o : o + 1]
             sig = 1.0 / (1.0 + jnp.exp(-pre))
             act_ref[o, p] = (pre * sig).astype(BF16)
             row.append(go_ref[o, p].astype(F32) * (sig * (1.0 + pre * (1.0 - sig))))
         grads.append(jnp.concatenate(row, axis=0).astype(BF16))
         gb[0, p, x, h, gx_.z4, k] = grads[p]
 
-    gg_.borders()
     gg_.z_send(0)
 
     plain = jnp.concatenate(grads, axis=1).astype(F32)
@@ -279,7 +309,7 @@
     per_o = jnp.sum(plain.reshape(4, 8, 256), axis=(1, 2), keepdims=True).reshape(4, 1)
     sums.append(jnp.broadcast_to(per_o, (4, 256)))
     sums.append(jnp.zeros((16, 256), F32))
-    dw[...] = jnp.concatenate(sums, axis=0).reshape(4, 32, 256)
+    dw[...] = jnp.concatenate(sums, axis=0).reshape(4, 32, 256).astype(BF16)
     for m in range(1, NY):
         copies.send(dw.at[(y + m) % NY], yb.at[y], sy.at[y], at((y + m) % NY, zh))
 
@@ -289,101 +319,115 @@
     yb[y] = dw[y]
     for m in range(1, NY):
         landed(yb.at[(y + m) % NY], sy.at[(y + m) % NY])
-    zb[zh] = (yb[0] + yb[1] + yb[2] + yb[3]).astype(BF16)
+    zb[zh] = sum(yb[m].astype(F32) for m in range(NY)).astype(BF16)
     for s in (1, NH - 1):
         copies.send(zb.at[zh], zb.at[zh], sz.at[zh], at(y, (zh + s) % NH))
 
     gg_.x_near(0, h)
-    gg_.wait_borders()
-    gg_.z_send(1)
     gg_.z_far(0)
     gg_.x_send(0, f)
+
+    landed(t4, s3)
+    all_rows[0:256, :] = t3[...].astype(F32).reshape(256, 128)
+    all_rows[256:512, :] = t4[...].astype(F32).reshape(256, 128)
+    turned_weights(all_rows, spread, wide, k)
+    band_weights(wide, wb, lambda t, j: t % 4 * 32 + t // 12 * 9 + j * 3 + t % 12 // 4, -1)
+
     gg_.x_far(0, h)
-    gg_.z_mates(1)
-    gg_.x_send(1, h)
-    gg_.z_mirror(1)
     gg_.x_near(0, f)
     for s in (1, NH - 1):
         landed(zb.at[(zh + s) % NH], sz.at[(zh + s) % NH])
     source, target = (zh + 3 + 2 * k) % NH, (zh + 1 + 2 * k) % NH
     copies.send(zb.at[source], zb.at[source], sz.at[source], at(y, target))
     gg_.x_far(0, f)
-    gg_.x_near(1, h)
-    gg_.z_far(1)
-    gg_.x_send(1, f)
-    gg_.x_far(1, h)
-    gg_.x_near(1, f)
     gg_.c_wait(0)
     own2 = jnp.dot(wb[...], gg_.pair(0), preferred_element_type=F32)
+    for c in range(4):
+        po[0, c] = turned_sum(lambda l: part(own2, 2, l, c, 1), -1).astype(BF16)
+        po[1, c] = turned_sum(lambda l: part(own2, 0, l, c, 0), -1).astype(BF16)
+    copies.send(po.at[0], pi.at[0], sp.at[0], after)
+    copies.send(po.at[1], pi.at[1], sp.at[1], before)
     landed(zb.at[(zh + 2) % NH], sz.at[(zh + 2) % NH])
-    total = zb[0].astype(F32) + zb[1].astype(F32) + zb[2].astype(F32) + zb[3].astype(F32)
-    tot[y] = total * scale
+    tot[y] = sum(zb[m].astype(F32) for m in range(NH)) * scale
     for m in range(1, NY):
         copies.send(tot.at[y], tot.at[y], sg.at[y], at((y + m) % NY, zh))
-    gg_.x_far(1, f)
-    gg_.c_wait(1)
-    rim2 = jnp.dot(wb[...], gg_.pair(1), preferred_element_type=F32)
     for p in range(2):
+        landed(pi.at[p], sp.at[p])
         for c in range(4):
-            out = jnp.zeros((8, 128), F32)
-            for l in range(3):
-                if p == 0:
-                    term = part(own2, 0, l, c, 1) + part(own2, 1, l, c, 0) + part(rim2, 2, l, c, 0)
-                else:
-                    term = part(rim2, 0, l, c, 1) + part(own2, 1, l, c, 1) + part(own2, 2, l, c, 0)
-                out += term if l == 1 else pltpu.roll(term, (l - 1) % 128, 1)
-            ig_ref[c, p] = out.astype(BF16)
+            if p == 0:
+                terms = lambda l: part(own2, 0, l, c, 1) + part(own2, 1, l, c, 0)
+            else:
+                terms = lambda l: part(own2, 1, l, c, 1) + part(own2, 2, l, c, 0)
+            ig_ref[c, p] = (turned_sum(terms, -1) + pi[p, c].astype(F32)).astype(BF16)
     for m in range(1, NY):
         landed(tot.at[(y + m) % NY], sg.at[(y + m) % NY])
-    everything = tot[...].reshape(128, 256)
+    out_ref[...] = tot[...].reshape(128, 256)
+    copies.drain()
+
+
+def finish(act_in, ig_in, sums, act_ref, ig_ref, wg_ref, bg_ref):
+    act_ref[...] = act_in[...]
+    ig_ref[...] = ig_in[...]
     for t in range(27):
-        wg_ref[t] = everything[4 * t : 4 * t + 4]
-    bg_ref[...] = everything[108:112, :128]
-    copies.drain()
+        wg_ref[t] = sums[4 * t : 4 * t + 4, :]
+    tail = sums[104:112, 0:128]
+    lane = lax.broadcasted_iota(jnp.int32, (8, 128), 1)
+    sub = lax.broadcasted_iota(jnp.int32, (8, 128), 0)
+    bg_ref[...] = jnp.sum(jnp.where(sub == lane + 4, tail, 0.0), axis=0, keepdims=True)[:, 0:4]
 
 
 def on_device(x_in, weight, bias_vec, grad_out):
     n_cells = lax.axis_size("slab") * x_in.shape[1] * x_in.shape[2] * x_in.shape[3]
     scale = 1.0 / math.sqrt(n_cells)
-    planes = jnp.transpose(x_in, (1, 0, 2, 3)).reshape(2, 32, 128)
-    by_tap = jnp.transpose(weight, (1, 0, 2)).reshape(108, 256)
-    turned = jnp.pad(weight, ((0, 0), (0, 5), (0, 0))).reshape(128, 256).T.reshape(64, 4, 128)
-    turned = lax.all_to_all(turned, "chan", 0, 0, tiled=True)
-    turned = jnp.transpose(turned, (1, 0, 2))
     dma = lambda *shape: pltpu.SemaphoreType.DMA(shape)
-    gathered = pltpu.VMEM((2, 2, NX, 2, 4, NK, 32, 128), BF16)
     vmem = pl.BlockSpec(memory_space=pltpu.VMEM)
-    act, grad_in, filters, bias_grad = pl.pallas_call(
+    block = jax.ShapeDtypeStruct((4, 2, 8, 128), BF16)
+    act, grad_in, sums = pl.pallas_call(
         functools.partial(kernel, scale),
-        out_shape=(
-            jax.ShapeDtypeStruct((4, 2, 8, 128), BF16),
-            jax.ShapeDtypeStruct((4, 2, 8, 128), BF16),
-            jax.ShapeDtypeStruct((27, 4, 256), F32),
-            jax.ShapeDtypeStruct((4, 128), F32),
-        ),
-        in_specs=[vmem, vmem, vmem, pl.BlockSpec(memory_space=pltpu.SMEM), vmem],
-        out_specs=(vmem,) * 4,
+        out_shape=(block, block, jax.ShapeDtypeStruct((128, 256), F32)),
+        in_specs=[vmem] * 4,
+        out_specs=(vmem,) * 3,
         scratch_shapes=[
-            gathered,
-            gathered,
+            pltpu.VMEM((2, 2, NX, 2, 4, NK, 32, 128), BF16),
+            pltpu.VMEM((1, 2, NX, 2, 4, NK, 32, 128), BF16),
             pltpu.VMEM((256, 2048), BF16),
             pltpu.VMEM((128, 2048), F32),
+            pltpu.VMEM((16, 128, 128), F32),
             pltpu.VMEM((288, 2048), BF16),
             pltpu.VMEM((288, 2048), BF16),
             pltpu.VMEM((288, 2048), BF16),
-            pltpu.VMEM((4, 32, 256), F32),
-            pltpu.VMEM((4, 32, 256), F32),
+            pltpu.VMEM((128, 256), F32),
+            pltpu.VMEM((NX, NZ, 8, 128), BF16),
+            pltpu.VMEM((NZ, NX, 8, 128), BF16),
+            pltpu.VMEM((NX, NZ, 8, 128), BF16),
+            pltpu.VMEM((NX, NZ, 8, 128), BF16),
+            pltpu.VMEM((512, 128), F32),
+            pltpu.VMEM((4, 32, 256), BF16),
+            pltpu.VMEM((4, 32, 256), BF16),
             pltpu.VMEM((4, 32, 256), BF16),
             pltpu.VMEM((4, 32, 256), F32),
-            dma(100),
-            *([dma(2, 8), dma(2, 2, 4), dma(2, 2, 4), dma(2)] * 2),
-            dma(4),
-            dma(4),
-            dma(4),
+            pltpu.VMEM((2, 4, 8, 128), BF16),
+            pltpu.VMEM((2, 4, 8, 128), BF16),
+            dma(96),
+            dma(2, 8), dma(2, 2, 4), dma(2, 2, 4), dma(2),
+            dma(1, 8), dma(1, 2, 4), dma(1, 2, 4),
+            dma(8), dma(4), pltpu.SemaphoreType.DMA,
+            dma(4), dma(4), dma(4), dma(2),
         ],
         compiler_params=pltpu.CompilerParams(collective_id=0, has_side_effects=True),
-    )(planes, by_tap, turned, bias_vec.astype(F32), grad_out)
-    return (act, grad_in, jnp.transpose(filters, (1, 0, 2)), bias_grad[:, 0])
+    )(x_in, jnp.transpose(weight, (1, 0, 2)), bias_vec.reshape(1, 4), grad_out)
+    act, grad_in, filters, bias_grad = pl.pallas_call(
+        finish,
+        out_shape=(
+            block,
+            block,
+            jax.ShapeDtypeStruct((27, 4, 256), F32),
+            jax.ShapeDtypeStruct((1, 4), F32),
+        ),
+        in_specs=[vmem] * 3,
+        out_specs=(vmem,) * 4,
+    )(act, grad_in, sums)
+    return (act, grad_in, jnp.transpose(filters, (1, 0, 2)), bias_grad.reshape(4))
 
 
 def solution(mesh):

time: 116 us -> 90 us (0.78)
  starting transfers between devices: 18.3 us -> 0 us
  Pallas kernels: 76.8 us -> 89.1 us
  waiting for transfers between devices: 11.1 us -> 0 us
  local copies, waits for them, and re-layouts: 8.26 us -> 0 us
    all_to_all x1 -> x0, starting transfers between devices: 18.3 us -> none  [on_device(): turned = lax.all_to_all(turned, 'chan', 0, 0, tiled=True)]
    pallas_call x1 -> x2, Pallas kernels: 76.8 us -> 89.1 us  [the longest x1 87.5 us: on_device(): pl.pallas_call(functools.partial(kernel, scale), out_shape=(block, block,...]
    all_to_all x1 -> x0, waiting for transfers between devices: 11.1 us -> none  [on_device(): turned = lax.all_to_all(turned, 'chan', 0, 0, tiled=True)]
    unnamed x14 -> x0, local copies, waits for them, and re-layouts: 5.01 us -> none
    reshape x2 -> x0, local copies, waits for them, and re-layouts: 1.24 us -> none  [the longest x1 0.64 us: on_device(): by_tap = jnp.transpose(weight, (1, 0, 2)).reshape(108, 256)]
  transfers between devices with their start and end apart: 1 -> 0, of which waited for: 1 -> 0; matrix products, arithmetic and copies ran while one was open for 2% -> 0% of each run, Pallas kernels for 0% -> 0%
where the time goes in v2:
time: 90 us; the launch traced here: 89.8 us
  Pallas kernels  89.1 us (99%)
    pallas_call x1, Pallas kernels, on_device(): pl.pallas_call(functools.partial(kernel, scale), out_shape=(block, block,...  87.5 us

profile of v2, /device:TPU:1, one launch (start us, length us, event | category | flops | bytes accessed | tf_op | source)
XLA Modules:
  0.0 89.8 jit_solution(8667150883427209307)
XLA Ops:
  0.6 87.5 %shard_map.75 = (bf16[4,2,8,128]{3,2,1,0:T(8,128)(2,1)}, bf16[4,2,8,128]{3,2,1,0:T(8,128)(2,1)}, f32[128,256]{1,0:T(8,128)}) custom-call(bf16[4,2,8,128]{3,2,1,0:T(8,128)(2,1)} %x_ref.1, bf16[27,4,256]{2,1,0:T(4,128)(2,1)} %bitcast.4, bf16[1,4]{1,0:T(2,128)(2,1)} %bitcast.5, bf16[4,2,8,128]{3,2,1,0:T(8,128)(2,1)} %go_ref.1), custom_call_target="tpu_custom_call" | custom-call | tf_op jit(solution)/shard_map/pallas_call | solution.py:385
  88.2 1.6 %shard_map.76 = (bf16[4,2,8,128]{3,2,1,0:T(8,128)(2,1)}, bf16[4,2,8,128]{3,2,1,0:T(8,128)(2,1)}, f32[27,4,256]{2,1,0:T(4,128)}, f32[1,4]{1,0:T(1,128)}) custom-call(bf16[4,2,8,128]{3,2,1,0:T(8,128)(2,1)} %get-tuple-element.11.act_in, bf16[4,2,8,128]{3,2,1,0:T(8,128)(2,1)} %get-tuple-element.12.ig_in, f32[128,256]{1,0:T(8,128)} %get-tuple-element.13.sums), custom_call_target="tpu_custom_call" | custom-call | tf_op jit(solution)/shard_map/pallas_call | solution.py:419

commit v3 on v2

v3 whole, which is shorter than its diff:
```python
import functools
import math

import jax
import jax.numpy as jnp
from jax import lax
from jax.experimental import pallas as pl
from jax.experimental.pallas import tpu as pltpu
from jax.sharding import PartitionSpec as P

MESH = pl.DeviceIdType.MESH
F32, BF16 = jnp.float32, jnp.bfloat16
NX, NZ, NK = 4, 8, 2
NY, NH = 4, 4
NT = (((1,), (1,)), ((), ()))


class Copies:
    def __init__(self, send_sems):
        self.send_sems = send_sems
        self.started = []

    def send(self, src, dst, recv_sem, device):
        copy = pltpu.make_async_remote_copy(
            src_ref=src,
            dst_ref=dst,
            send_sem=self.send_sems.at[len(self.started)],
            recv_sem=recv_sem,
            device_id=device,
            device_id_type=MESH,
        )
        copy.start()
        self.started.append(copy)

    def drain(self):
        for copy in self.started:
            copy.wait_send()


def landed(dst, recv_sem):
    here = (lax.axis_index("slab"), lax.axis_index("chan"))
    pltpu.make_async_remote_copy(
        src_ref=dst, dst_ref=dst, send_sem=recv_sem, recv_sem=recv_sem, device_id=here, device_id_type=MESH
    ).wait_recv()


class Gather:
    def __init__(self, copies, place, buf, rz, rx, rc):
        self.c = copies
        self.slab, self.x, self.z, self.k = place
        self.h, self.z4 = self.z // 4, self.z % 4
        self.f = 1 - self.h
        self.mates = [(self.z4 + m) % 4 for m in range(1, 4)]
        self.near_x = [(self.x + step) % 4 for step in (1, 3)]
        self.far_x = (self.x + 2) % 4
        self.buf, self.rz, self.rx, self.rc = buf, rz, rx, rc

    def dev(self, x, z, k):
        return (self.slab, (x * NZ + z) * NK + k)

    def block(self, x, h, z4, k):
        return self.buf.at[:, x, h, z4, k]

    def unit(self, x, z4, k):
        if z4 is None:
            return self.buf.at[:, x, self.h, :, k], 4
        return self.buf.at[:, x, self.f, z4, k], z4

    def z_send(self):
        mine = self.block(self.x, self.h, self.z4, self.k)
        for mate in self.mates:
            self.c.send(mine, mine, self.rz.at[self.z], self.dev(self.x, self.h * 4 + mate, self.k))
        self.c.send(mine, mine, self.rz.at[self.z], self.dev(self.x, self.f * 4 + self.z4, self.k))

    def z_mates(self):
        for mate in self.mates:
            landed(self.block(self.x, self.h, mate, self.k), self.rz.at[self.h * 4 + mate])
        self.x_send(None)

    def z_mirror(self):
        other = self.f * 4 + self.z4
        theirs = self.block(self.x, self.f, self.z4, self.k)
        landed(theirs, self.rz.at[other])
        for mate in self.mates:
            self.c.send(theirs, theirs, self.rz.at[other], self.dev(self.x, self.h * 4 + mate, self.k))
        self.x_send(self.z4)

    def z_far(self):
        for mate in self.mates:
            landed(self.block(self.x, self.f, mate, self.k), self.rz.at[self.f * 4 + mate])
            self.x_send(mate)

    def c_send(self, x, z4):
        mine, at = self.unit(x, z4, self.k)
        self.c.send(mine, mine, self.rc.at[at, x], self.dev(self.x, self.z, 1 - self.k))

    def x_send(self, z4):
        mine, at = self.unit(self.x, z4, self.k)
        for x in self.near_x:
            self.c.send(mine, mine, self.rx.at[at, self.x], self.dev(x, self.z, self.k))
        self.c_send(self.x, z4)

    def x_near(self, z4):
        for x in self.near_x:
            theirs, at = self.unit(x, z4, self.k)
            landed(theirs, self.rx.at[at, x])
        source, target = (self.x + 3 + 2 * self.k) % 4, (self.x + 1 + 2 * self.k) % 4
        passed, at = self.unit(source, z4, self.k)
        self.c.send(passed, passed, self.rx.at[at, source], self.dev(target, self.z, self.k))
        for x in self.near_x:
            self.c_send(x, z4)

    def x_far(self, z4):
        theirs, at = self.unit(self.far_x, z4, self.k)
        landed(theirs, self.rx.at[at, self.far_x])
        self.c_send(self.far_x, z4)

    def c_wait(self):
        for z4 in (None, self.z4, *self.mates):
            for x in range(4):
                theirs, at = self.unit(x, z4, 1 - self.k)
                landed(theirs, self.rc.at[at, x])

    def pair(self):
        return jnp.concatenate([self.buf[p].reshape(2048, 128) for p in range(2)], axis=1)


def band_weights(expanded, out, row_of, sign):
    lane = lax.broadcasted_iota(jnp.int32, (8, 2048), 1)
    sub = lax.broadcasted_iota(jnp.int32, (8, 2048), 0)
    tap = (sign * (lane - sub) + 1) & 7

    def one(t):
        rows = [expanded[pl.ds(row_of(t, j), 1), :] for j in range(3)]
        return jnp.where(tap == 0, rows[0], jnp.where(tap == 1, rows[1], jnp.where(tap == 2, rows[2], 0.0)))

    def body(u, carry):
        both = jnp.concatenate([one(2 * u), one(2 * u + 1)], axis=0)
        out[pl.ds(pl.multiple_of(16 * u, 16), 16), :] = both.astype(BF16)
        return carry

    lax.fori_loop(0, 18, body, 0)


def turned_weights(all_rows, spread, wide, k):
    row = lax.broadcasted_iota(jnp.int32, (64, 256), 0)
    col = lax.broadcasted_iota(jnp.int32, (64, 256), 1)
    source = jnp.where(row < 32, 2 * row + k, 2 * row - 63 - k)
    within = lax.broadcasted_iota(jnp.int32, (27, 128), 1) // 8 % 4
    for c in range(4):
        low, high = [all_rows[pl.ds(4 * q + c, 64, stride=8), :] for q in range(2)]
        mine = jnp.where(k == 0, low, high).T.astype(BF16)
        for n in range(8):
            pick = jnp.where(source == 8 * n + (col >> 5), 1.0, 0.0).astype(BF16)
            full = jnp.dot(mine, pick, preferred_element_type=F32)
            for half in range(2):
                spread[2 * n + half] = full[:, 128 * half : 128 * half + 128]
                total = spread[2 * n + half, pl.ds(0, 27, stride=4), :]
                for o in range(1, 4):
                    total = jnp.where(within == o, spread[2 * n + half, pl.ds(o, 27, stride=4), :], total)
                wide[32 * c : 32 * c + 27, 256 * n + 128 * half : 256 * n + 128 * half + 128] = total


def kernel(
    scale,
    x_hbm, w_hbm, bias_hbm, go_hbm,
    act_ref, ig_ref, out_ref,
    x_ref, w_ref, bias_ref, go_ref, load_sems,
    xb, gb, rep, wide, spread, wa, wb, dm, rows, t1, t2, t3, t4, all_rows, dw, yb, zb, tot, po, pi, fo, fi, go_rim,
    send_sems, xz, xx, xc, gz, gx, gc, s1, s2, s3, sy, sz, sg, sp, sf, so,
):
    slab, chan = lax.axis_index("slab"), lax.axis_index("chan")
    y, zh = slab // NH, slab % NH
    x, z, k = chan // (NZ * NK), chan // NK % NZ, chan % NK
    place = (slab, x, z, k)
    copies = Copies(send_sems)
    gx_ = Gather(copies, place, xb, xz, xx, xc)
    gg_ = Gather(copies, place, gb, gz, gx, gc)
    h = gx_.h
    at = lambda yy, hh: (yy * NH + hh, chan)
    line = [(z + m) % NZ for m in range(1, NZ)]
    ring = [(x + m) % NX for m in range(1, NX)]
    after, before = ((slab + 1) % (NY * NH), chan), ((slab + NY * NH - 1) % (NY * NH), chan)

    partners = [gx_.dev(x, z, 1 - k)]
    partners += [gx_.dev(xx_, z, k) for xx_ in ring]
    partners += [gx_.dev(x, zz, k) for zz in line]
    partners += [at((y + m) % NY, zh) for m in range(1, NY)]
    partners += [at(y, (zh + s) % NH) for s in (1, NH - 1)]
    partners += [after, before]
    barrier = pltpu.get_barrier_semaphore()
    for partner in partners:
        pl.semaphore_signal(barrier, inc=1, device_id=partner, device_id_type=MESH)

    loads = [
        pltpu.make_async_copy(source, target, load_sems.at[n])
        for n, (source, target) in enumerate(
            ((w_hbm, w_ref), (x_hbm, x_ref), (go_hbm, go_ref), (bias_hbm, bias_ref))
        )
    ]
    for load in loads:
        load.start()
    for n in range(8):
        row = lax.broadcasted_iota(jnp.int32, (256, 256), 0)
        col = lax.broadcasted_iota(jnp.int32, (256, 256), 1)
        rep[:, 256 * n : 256 * n + 256] = jnp.where(row == 32 * n + (col >> 3), 1.0, 0.0).astype(BF16)
    for load in loads:
        load.wait()
    for p in range(2):
        xb[p, x, h, gx_.z4, k] = x_ref[:, p].astype(F32).reshape(32, 128).astype(BF16)
    rows[104:128, :] = jnp.zeros((24, 256), F32)
    for t in range(27):
        rows[4 * t : 4 * t + 4, :] = w_ref[t].astype(F32)
    t1[...] = rows[...].T.reshape(4, 8, 8, 128).astype(BF16)
    by_tap = rows[...].astype(BF16)
    for n in range(8):
        wide[:, 256 * n : 256 * n + 256] = jnp.dot(
            by_tap, rep[:, 256 * n : 256 * n + 256], preferred_element_type=F32
        )
    band_weights(wide, wa, lambda t, j: t // 12 * 36 + j * 12 + t % 12, 1)

    pl.semaphore_wait(barrier, len(partners))
    gx_.z_send()
    gx_.z_mates()
    gx_.z_mirror()
    gx_.x_near(None)
    gx_.z_far()
    copies.send(go_ref.at[:, 1], go_rim.at[0], so.at[0], after)
    copies.send(go_ref.at[:, 0], go_rim.at[1], so.at[1], before)
    for zz in line:
        copies.send(t1.at[:, zz], t2.at[z], s1.at[z], gx_.dev(x, zz, k))
    t2[z] = t1[:, z]
    gx_.x_near(gx_.z4)
    gx_.x_far(None)
    for mate in gx_.mates:
        gx_.x_near(mate)
    gx_.x_far(gx_.z4)
    for mate in gx_.mates:
        gx_.x_far(mate)
    gx_.c_wait()

    own = jnp.dot(wa[...], gx_.pair(), preferred_element_type=F32)

    def part(value, i, l, o, p):
        base = ((i * 3 + l) * 4 + o) * 8
        return value[base : base + 8, 128 * p : 128 * p + 128]

    def turned_sum(terms, sign):
        total = None
        for l in range(3):
            term = terms(l)
            term = term if l == 1 else pltpu.roll(term, sign * (1 - l) % 128, 1)
            total = term if total is None else total + term
        return total

    shares = [
        [turned_sum(lambda l: part(own, 2, l, o, 0), 1) for o in range(4)],
        [turned_sum(lambda l: part(own, 1, l, o, 0) + part(own, 2, l, o, 1), 1) for o in range(4)],
        [turned_sum(lambda l: part(own, 0, l, o, 0) + part(own, 1, l, o, 1), 1) for o in range(4)],
        [turned_sum(lambda l: part(own, 0, l, o, 1), 1) for o in range(4)],
    ]
    for o in range(4):
        for n in range(4):
            fo[n, o] = shares[n][o].astype(BF16)
    copies.send(fo.at[2:4], fi.at[0:2], sf.at[0], after)
    copies.send(fo.at[0:2], fi.at[2:4], sf.at[1], before)

    for zz in line:
        landed(t2.at[zz], s1.at[zz])
    for xx_ in ring:
        copies.send(t2.at[:, xx_], t3.at[x], s2.at[x], gx_.dev(xx_, z, k))
    t3[x] = t2[:, x]
    for xx_ in ring:
        landed(t3.at[xx_], s2.at[xx_])
    copies.send(t3, t4, s3, gx_.dev(x, z, 1 - k))
    landed(t4, s3)
    all_rows[0:256, :] = t3[...].astype(F32).reshape(256, 128)
    all_rows[256:512, :] = t4[...].astype(F32).reshape(256, 128)
    turned_weights(all_rows, spread, wide, k)
    band_weights(wide, wb, lambda t, j: t % 4 * 32 + t // 12 * 9 + j * 3 + t % 12 // 4, -1)

    landed(fi.at[0:2], sf.at[0])
    landed(fi.at[2:4], sf.at[1])
    for side in range(2):
        landed(go_rim.at[side], so.at[side])
    offsets = bias_ref[...].astype(F32)
    grads = []
    for n in range(4):
        row = []
        for o in range(4):
            pre = shares[n][o] + fi[n, o].astype(F32) + offsets[:, o : o + 1]
            sig = 1.0 / (1.0 + jnp.exp(-pre))
            if n in (1, 2):
                act_ref[o, n - 1] = (pre * sig).astype(BF16)
                given = go_ref[o, n - 1]
            else:
                given = go_rim[n // 3, o]
            row.append(given.astype(F32) * (sig * (1.0 + pre * (1.0 - sig))))
        grads.append(jnp.concatenate(row, axis=0).astype(BF16))
    gb[0, x, h, gx_.z4, k] = grads[1]
    gb[1, x, h, gx_.z4, k] = grads[2]

    gg_.z_send()

    grads = [g.astype(F32) for g in grads]
    turns = [[g if l == 1 else pltpu.roll(g, (l - 1) % 128, 1) for l in range(3)] for g in grads]
    rolled = jnp.concatenate(
        [jnp.concatenate([turns[2 - i][l], turns[3 - i][l]], axis=1) for i in range(3) for l in range(3)], axis=0
    ).astype(BF16)
    lane = lax.broadcasted_iota(jnp.int32, (8, 2048), 1)
    sub = lax.broadcasted_iota(jnp.int32, (8, 2048), 0)
    tap = (lane - sub + 1) & 7
    whole = lax.dot_general(rolled, gx_.pair(), NT, preferred_element_type=F32)
    sums = []
    for i in range(3):
        full = whole[96 * i : 96 * i + 96].reshape(12, 8, 2048)
        for j in range(3):
            kept = jnp.where((tap == j)[None], full, 0.0)
            dm[96 * j : 96 * j + 96, :] = kept.reshape(96, 2048).astype(BF16)
        folded = lax.dot_general(dm[...], rep[...], NT, preferred_element_type=F32)
        sums.append(jnp.sum(folded.reshape(36, 8, 256), axis=1))
    per_o = jnp.sum((grads[1] + grads[2]).reshape(4, 8, 128), axis=(1, 2), keepdims=True).reshape(4, 1)
    sums.append(jnp.broadcast_to(per_o, (4, 256)))
    sums.append(jnp.zeros((16, 256), F32))
    dw[...] = jnp.concatenate(sums, axis=0).reshape(4, 32, 256).astype(BF16)
    for m in range(1, NY):
        copies.send(dw.at[(y + m) % NY], yb.at[y], sy.at[y], at((y + m) % NY, zh))

    gg_.z_mates()
    gg_.z_mirror()
    yb[y] = dw[y]
    for m in range(1, NY):
        landed(yb.at[(y + m) % NY], sy.at[(y + m) % NY])
    zb[zh] = sum(yb[m].astype(F32) for m in range(NY)).astype(BF16)
    for s in (1, NH - 1):
        copies.send(zb.at[zh], zb.at[zh], sz.at[zh], at(y, (zh + s) % NH))

    gg_.x_near(None)
    gg_.z_far()
    gg_.x_near(gg_.z4)
    gg_.x_far(None)
    for mate in gg_.mates:
        gg_.x_near(mate)
    for s in (1, NH - 1):
        landed(zb.at[(zh + s) % NH], sz.at[(zh + s) % NH])
    source, target = (zh + 3 + 2 * k) % NH, (zh + 1 + 2 * k) % NH
    copies.send(zb.at[source], zb.at[source], sz.at[source], at(y, target))
    gg_.x_far(gg_.z4)
    for mate in gg_.mates:
        gg_.x_far(mate)
    gg_.c_wait()
    own2 = jnp.dot(wb[...], gg_.pair(), preferred_element_type=F32)
    for c in range(4):
        po[0, c] = turned_sum(lambda l: part(own2, 2, l, c, 1), -1).astype(BF16)
        po[1, c] = turned_sum(lambda l: part(own2, 0, l, c, 0), -1).astype(BF16)
    copies.send(po.at[0], pi.at[0], sp.at[0], after)
    copies.send(po.at[1], pi.at[1], sp.at[1], before)
    landed(zb.at[(zh + 2) % NH], sz.at[(zh + 2) % NH])
    tot[y] = sum(zb[m].astype(F32) for m in range(NH)) * scale
    for m in range(1, NY):
        copies.send(tot.at[y], tot.at[y], sg.at[y], at((y + m) % NY, zh))
    for p in range(2):
        landed(pi.at[p], sp.at[p])
        for c in range(4):
            if p == 0:
                terms = lambda l: part(own2, 0, l, c, 1) + part(own2, 1, l, c, 0)
            else:
                terms = lambda l: part(own2, 1, l, c, 1) + part(own2, 2, l, c, 0)
            ig_ref[c, p] = (turned_sum(terms, -1) + pi[p, c].astype(F32)).astype(BF16)
    for m in range(1, NY):
        landed(tot.at[(y + m) % NY], sg.at[(y + m) % NY])
    out_ref[...] = tot[...].reshape(128, 256)
    copies.drain()


def finish(act_in, ig_in, sums, act_ref, ig_ref, wg_ref, bg_ref):
    act_ref[...] = act_in[...]
    ig_ref[...] = ig_in[...]
    for t in range(27):
        wg_ref[t] = sums[4 * t : 4 * t + 4, :]
    tail = sums[104:112, 0:128]
    lane = lax.broadcasted_iota(jnp.int32, (8, 128), 1)
    sub = lax.broadcasted_iota(jnp.int32, (8, 128), 0)
    bg_ref[...] = jnp.sum(jnp.where(sub == lane + 4, tail, 0.0), axis=0, keepdims=True)[:, 0:4]


def on_device(x_in, weight, bias_vec, grad_out):
    n_cells = lax.axis_size("slab") * x_in.shape[1] * x_in.shape[2] * x_in.shape[3]
    scale = 1.0 / math.sqrt(n_cells)
    dma = lambda *shape: pltpu.SemaphoreType.DMA(shape)
    vmem, anywhere = pl.BlockSpec(memory_space=pltpu.VMEM), pl.BlockSpec(memory_space=pl.ANY)
    held = lambda *args: pltpu.with_memory_space_constraint(*args, pltpu.VMEM)
    block = jax.ShapeDtypeStruct((4, 2, 8, 128), BF16)
    act, grad_in, sums = pl.pallas_call(
        functools.partial(kernel, scale),
        out_shape=(
            pltpu.VMEM((4, 2, 8, 128), BF16),
            pltpu.VMEM((4, 2, 8, 128), BF16),
            pltpu.VMEM((128, 256), F32),
        ),
        in_specs=[anywhere] * 4,
        out_specs=(vmem,) * 3,
        scratch_shapes=[
            pltpu.VMEM((4, 2, 8, 128), BF16),
            pltpu.VMEM((27, 4, 256), BF16),
            pltpu.VMEM((1, 4), BF16),
            pltpu.VMEM((4, 2, 8, 128), BF16),
            dma(4),
            pltpu.VMEM((2, NX, 2, 4, NK, 32, 128), BF16),
            pltpu.VMEM((2, NX, 2, 4, NK, 32, 128), BF16),
            pltpu.VMEM((256, 2048), BF16),
            pltpu.VMEM((128, 2048), F32),
            pltpu.VMEM((16, 128, 128), F32),
            pltpu.VMEM((288, 2048), BF16),
            pltpu.VMEM((288, 2048), BF16),
            pltpu.VMEM((288, 2048), BF16),
            pltpu.VMEM((128, 256), F32),
            pltpu.VMEM((NX, NZ, 8, 128), BF16),
            pltpu.VMEM((NZ, NX, 8, 128), BF16),
            pltpu.VMEM((NX, NZ, 8, 128), BF16),
            pltpu.VMEM((NX, NZ, 8, 128), BF16),
            pltpu.VMEM((512, 128), F32),
            pltpu.VMEM((4, 32, 256), BF16),
            pltpu.VMEM((4, 32, 256), BF16),
            pltpu.VMEM((4, 32, 256), BF16),
            pltpu.VMEM((4, 32, 256), F32),
            pltpu.VMEM((2, 4, 8, 128), BF16),
            pltpu.VMEM((2, 4, 8, 128), BF16),
            pltpu.VMEM((4, 4, 8, 128), BF16),
            pltpu.VMEM((4, 4, 8, 128), BF16),
            pltpu.VMEM((2, 4, 8, 128), BF16),
            dma(120),
            dma(8), dma(5, 4), dma(5, 4),
            dma(8), dma(5, 4), dma(5, 4),
            dma(8), dma(4), pltpu.SemaphoreType.DMA,
            dma(4), dma(4), dma(4), dma(2), dma(2), dma(2),
        ],
        compiler_params=pltpu.CompilerParams(collective_id=0, has_side_effects=True),
    )(x_in, jnp.transpose(weight, (1, 0, 2)), bias_vec.reshape(1, 4), grad_out)
    act, grad_in, filters, bias_grad = pl.pallas_call(
        finish,
        out_shape=(
            block,
            block,
            jax.ShapeDtypeStruct((27, 4, 256), F32),
            jax.ShapeDtypeStruct((1, 4), F32),
        ),
        in_specs=[vmem] * 3,
        out_specs=(vmem,) * 4,
    )(held(act), held(grad_in), held(sums))
    return (act, grad_in, jnp.transpose(filters, (1, 0, 2)), bias_grad.reshape(4))


def solution(mesh):
    placed = (
        P("chan", "slab", None, None),
        P("chan", None, None),
        P("chan"),
        P("chan", "slab", None, None),
    )
    return jax.shard_map(
        on_device,
        mesh=mesh,
        in_specs=placed,
        out_specs=(
            P("chan", "slab", None, None),
            P("chan", "slab", None, None),
            P("chan", None, None),
            P("chan"),
        ),
        check_vma=False,
    )
```

time: 90 us -> 81.9 us (0.910)
  Pallas kernels: 89.1 us -> 81 us
    pallas_call x1, Pallas kernels: 87.5 us -> 80.4 us  [on_device(): pl.pallas_call(functools.partial(kernel, scale), out_shape=(pltpu.VMEM((4...]
    pallas_call x1, Pallas kernels: 1.61 us -> 0.67 us  [on_device(): pl.pallas_call(finish, out_shape=(block, block, jax.ShapeDtypeStruct((27,...]
where the time goes in v3:
time: 81.9 us; the launch traced here: 81.7 us
  Pallas kernels  81 us (99%)
    pallas_call x1, Pallas kernels, on_device(): pl.pallas_call(functools.partial(kernel, scale), out_shape=(pltpu.VMEM((4...  80.4 us

profile of v3, /device:TPU:1, one launch (start us, length us, event | category | flops | bytes accessed | tf_op | source)
XLA Modules:
  0.0 81.7 jit_solution(17269867212191929532)
XLA Ops:
  0.6 80.4 %shard_map.75 = (bf16[4,2,8,128]{3,2,1,0:T(8,128)(2,1)S(1)}, bf16[4,2,8,128]{3,2,1,0:T(8,128)(2,1)S(1)}, f32[128,256]{1,0:T(8,128)S(1)}) custom-call(bf16[4,2,8,128]{3,2,1,0:T(8,128)(2,1)} %x_hbm.1, bf16[27,4,256]{2,1,0:T(4,128)(2,1)} %bitcast.4, bf16[1,4]{1,0:T(2,128)(2,1)} %bitcast.5, bf16[4,2,8,128]{3,2,1,0:T(8,128)(2,1)} %go_hbm.1), custom_call_target="tpu_custom_call" | custom-call | tf_op jit(solution)/shard_map/pallas_call | solution.py:394
  81.0 0.7 shard_map.76

commit v4 on v3

--- a/solution.py
+++ b/solution.py
@@ -35,6 +35,7 @@
     def drain(self):
         for copy in self.started:
             copy.wait_send()
+        self.started = []
 
 
 def landed(dst, recv_sem):
@@ -45,7 +46,7 @@
 
 
 class Gather:
-    def __init__(self, copies, place, buf, rz, rx, rc):
+    def __init__(self, copies, place, buf, rz, rn, rf, rc):
         self.c = copies
         self.slab, self.x, self.z, self.k = place
         self.h, self.z4 = self.z // 4, self.z % 4
@@ -53,7 +54,7 @@
         self.mates = [(self.z4 + m) % 4 for m in range(1, 4)]
         self.near_x = [(self.x + step) % 4 for step in (1, 3)]
         self.far_x = (self.x + 2) % 4
-        self.buf, self.rz, self.rx, self.rc = buf, rz, rx, rc
+        self.buf, self.rz, self.rn, self.rf, self.rc = buf, rz, rn, rf, rc
 
     def dev(self, x, z, k):
         return (self.slab, (x * NZ + z) * NK + k)
@@ -61,10 +62,13 @@
     def block(self, x, h, z4, k):
         return self.buf.at[:, x, h, z4, k]
 
-    def unit(self, x, z4, k):
+    def half(self, x, h, k):
+        return self.buf.at[:, x, h, :, k]
+
+    def unit(self, x, z4):
         if z4 is None:
-            return self.buf.at[:, x, self.h, :, k], 4
-        return self.buf.at[:, x, self.f, z4, k], z4
+            return self.half(x, self.h, self.k), 4
+        return self.block(x, self.f, z4, self.k), z4
 
     def z_send(self):
         mine = self.block(self.x, self.h, self.z4, self.k)
@@ -76,6 +80,7 @@
         for mate in self.mates:
             landed(self.block(self.x, self.h, mate, self.k), self.rz.at[self.h * 4 + mate])
         self.x_send(None)
+        self.c_send(self.x, self.h)
 
     def z_mirror(self):
         other = self.f * 4 + self.z4
@@ -89,37 +94,36 @@
         for mate in self.mates:
             landed(self.block(self.x, self.f, mate, self.k), self.rz.at[self.f * 4 + mate])
             self.x_send(mate)
-
-    def c_send(self, x, z4):
-        mine, at = self.unit(x, z4, self.k)
-        self.c.send(mine, mine, self.rc.at[at, x], self.dev(self.x, self.z, 1 - self.k))
+        self.c_send(self.x, self.f)
+
+    def c_send(self, x, h):
+        mine = self.half(x, h, self.k)
+        self.c.send(mine, mine, self.rc, self.dev(self.x, self.z, 1 - self.k))
 
     def x_send(self, z4):
-        mine, at = self.unit(self.x, z4, self.k)
+        mine, at = self.unit(self.x, z4)
+        for way, x in enumerate(self.near_x):
+            self.c.send(mine, mine, self.rn.at[at, way], self.dev(x, self.z, self.k))
+
+    def x_near(self, z4):
+        for way, x in enumerate(self.near_x):
+            theirs, at = self.unit(x, z4)
+            landed(theirs, self.rn.at[at, 1 - way])
+        source, target = (self.x + 3 + 2 * self.k) % 4, (self.x + 1 + 2 * self.k) % 4
+        passed, _ = self.unit(source, z4)
+        self.c.send(passed, passed, self.rf.at[0 if z4 is None else 1], self.dev(target, self.z, self.k))
+
+    def near_to_core(self, h):
         for x in self.near_x:
-            self.c.send(mine, mine, self.rx.at[at, self.x], self.dev(x, self.z, self.k))
-        self.c_send(self.x, z4)
-
-    def x_near(self, z4):
-        for x in self.near_x:
-            theirs, at = self.unit(x, z4, self.k)
-            landed(theirs, self.rx.at[at, x])
-        source, target = (self.x + 3 + 2 * self.k) % 4, (self.x + 1 + 2 * self.k) % 4
-        passed, at = self.unit(source, z4, self.k)
-        self.c.send(passed, passed, self.rx.at[at, source], self.dev(target, self.z, self.k))
-        for x in self.near_x:
-            self.c_send(x, z4)
-
-    def x_far(self, z4):
-        theirs, at = self.unit(self.far_x, z4, self.k)
-        landed(theirs, self.rx.at[at, self.far_x])
-        self.c_send(self.far_x, z4)
+            self.c_send(x, h)
+
+    def x_far(self, n):
+        h = (self.h, self.f)[n]
+        landed(self.half(self.far_x, h, self.k), self.rf.at[n])
+        self.c_send(self.far_x, h)
 
     def c_wait(self):
-        for z4 in (None, self.z4, *self.mates):
-            for x in range(4):
-                theirs, at = self.unit(x, z4, 1 - self.k)
-                landed(theirs, self.rc.at[at, x])
+        landed(self.buf.at[:, :, :, :, 1 - self.k], self.rc)
 
     def pair(self):
         return jnp.concatenate([self.buf[p].reshape(2048, 128) for p in range(2)], axis=1)
@@ -167,30 +171,39 @@
     act_ref, ig_ref, out_ref,
     x_ref, w_ref, bias_ref, go_ref, load_sems,
     xb, gb, rep, wide, spread, wa, wb, dm, rows, t1, t2, t3, t4, all_rows, dw, yb, zb, tot, po, pi, fo, fi, go_rim,
-    send_sems, xz, xx, xc, gz, gx, gc, s1, s2, s3, sy, sz, sg, sp, sf, so,
+    send_sems, xz, xn, xf, xc, gz, gn, gf, gc, s1, s2, s3, sy, sz, sg, sp, sf, so, ready,
 ):
     slab, chan = lax.axis_index("slab"), lax.axis_index("chan")
     y, zh = slab // NH, slab % NH
     x, z, k = chan // (NZ * NK), chan // NK % NZ, chan % NK
     place = (slab, x, z, k)
     copies = Copies(send_sems)
-    gx_ = Gather(copies, place, xb, xz, xx, xc)
-    gg_ = Gather(copies, place, gb, gz, gx, gc)
+    gx_ = Gather(copies, place, xb, xz, xn, xf, xc)
+    gg_ = Gather(copies, place, gb, gz, gn, gf, gc)
     h = gx_.h
     at = lambda yy, hh: (yy * NH + hh, chan)
     line = [(z + m) % NZ for m in range(1, NZ)]
     ring = [(x + m) % NX for m in range(1, NX)]
     after, before = ((slab + 1) % (NY * NH), chan), ((slab + NY * NH - 1) % (NY * NH), chan)
 
+    def signal(sem, device):
+        pl.semaphore_signal(sem, inc=1, device_id=device, device_id_type=MESH)
+
     partners = [gx_.dev(x, z, 1 - k)]
     partners += [gx_.dev(xx_, z, k) for xx_ in ring]
-    partners += [gx_.dev(x, zz, k) for zz in line]
+    partners += [gx_.dev(x, h * 4 + m, k) for m in gx_.mates] + [gx_.dev(x, gx_.f * 4 + gx_.z4, k)]
     partners += [at((y + m) % NY, zh) for m in range(1, NY)]
-    partners += [at(y, (zh + s) % NH) for s in (1, NH - 1)]
-    partners += [after, before]
     barrier = pltpu.get_barrier_semaphore()
     for partner in partners:
-        pl.semaphore_signal(barrier, inc=1, device_id=partner, device_id_type=MESH)
+        signal(barrier, partner)
+    greets = {0: [at(y, 1), at(y, 3), at((y + NY - 1) % NY, 3)], 1: [at(y, 2)], 3: [at(y, 2)]}
+    answers = {1: [at(y, 0)], 2: [at(y, 1), at(y, 3)], 3: [at(y, 0), at((y + 1) % NY, 0)]}
+    for who, devices in greets.items():
+
+        @pl.when(zh == who)
+        def _(devices=devices):
+            for device in devices:
+                signal(barrier, device)
 
     loads = [
         pltpu.make_async_copy(source, target, load_sems.at[n])
@@ -219,24 +232,38 @@
         )
     band_weights(wide, wa, lambda t, j: t // 12 * 36 + j * 12 + t % 12, 1)
 
-    pl.semaphore_wait(barrier, len(partners))
+    pl.semaphore_wait(barrier, len(partners) + jnp.where(zh == 0, 0, jnp.where(zh == 1, 1, 2)))
+    for who, devices in answers.items():
+
+        @pl.when(zh == who)
+        def _(devices=devices):
+            for device in devices:
+                signal(ready, device)
+
     gx_.z_send()
     gx_.z_mates()
     gx_.z_mirror()
     gx_.x_near(None)
+    gx_.near_to_core(h)
     gx_.z_far()
-    copies.send(go_ref.at[:, 1], go_rim.at[0], so.at[0], after)
-    copies.send(go_ref.at[:, 0], go_rim.at[1], so.at[1], before)
     for zz in line:
         copies.send(t1.at[:, zz], t2.at[z], s1.at[z], gx_.dev(x, zz, k))
     t2[z] = t1[:, z]
     gx_.x_near(gx_.z4)
-    gx_.x_far(None)
+    gx_.x_far(0)
     for mate in gx_.mates:
         gx_.x_near(mate)
-    gx_.x_far(gx_.z4)
-    for mate in gx_.mates:
-        gx_.x_far(mate)
+    gx_.near_to_core(gx_.f)
+    gx_.x_far(1)
+
+    for who, devices in greets.items():
+
+        @pl.when(zh == who)
+        def _(devices=devices):
+            pl.semaphore_wait(ready, len(devices))
+
+    copies.send(go_ref.at[:, 1], go_rim.at[0], so.at[0], after)
+    copies.send(go_ref.at[:, 0], go_rim.at[1], so.at[1], before)
     gx_.c_wait()
 
     own = jnp.dot(wa[...], gx_.pair(), preferred_element_type=F32)
@@ -283,6 +310,7 @@
     landed(fi.at[2:4], sf.at[1])
     for side in range(2):
         landed(go_rim.at[side], so.at[side])
+    copies.drain()
     offsets = bias_ref[...].astype(F32)
     grads = []
     for n in range(4):
@@ -336,18 +364,18 @@
         copies.send(zb.at[zh], zb.at[zh], sz.at[zh], at(y, (zh + s) % NH))
 
     gg_.x_near(None)
+    gg_.near_to_core(h)
     gg_.z_far()
     gg_.x_near(gg_.z4)
-    gg_.x_far(None)
+    gg_.x_far(0)
     for mate in gg_.mates:
         gg_.x_near(mate)
+    gg_.near_to_core(gg_.f)
     for s in (1, NH - 1):
         landed(zb.at[(zh + s) % NH], sz.at[(zh + s) % NH])
     source, target = (zh + 3 + 2 * k) % NH, (zh + 1 + 2 * k) % NH
     copies.send(zb.at[source], zb.at[source], sz.at[source], at(y, target))
-    gg_.x_far(gg_.z4)
-    for mate in gg_.mates:
-        gg_.x_far(mate)
+    gg_.x_far(1)
     gg_.c_wait()
     own2 = jnp.dot(wb[...], gg_.pair(), preferred_element_type=F32)
     for c in range(4):
@@ -429,11 +457,12 @@
             pltpu.VMEM((4, 4, 8, 128), BF16),
             pltpu.VMEM((4, 4, 8, 128), BF16),
             pltpu.VMEM((2, 4, 8, 128), BF16),
-            dma(120),
-            dma(8), dma(5, 4), dma(5, 4),
-            dma(8), dma(5, 4), dma(5, 4),
+            dma(48),
+            dma(8), dma(5, 2), dma(2), pltpu.SemaphoreType.DMA,
+            dma(8), dma(5, 2), dma(2), pltpu.SemaphoreType.DMA,
             dma(8), dma(4), pltpu.SemaphoreType.DMA,
             dma(4), dma(4), dma(4), dma(2), dma(2), dma(2),
+            pltpu.SemaphoreType.REGULAR,
         ],
         compiler_params=pltpu.CompilerParams(collective_id=0, has_side_effects=True),
     )(x_in, jnp.transpose(weight, (1, 0, 2)), bias_vec.reshape(1, 4), grad_out)

time: 81.9 us -> 77.8 us (0.950)
  Pallas kernels: 81 us -> 76.9 us
    pallas_call x1, Pallas kernels: 80.4 us -> 76.3 us  [on_device(): pl.pallas_call(functools.partial(kernel, scale), out_shape=(pltpu.VMEM((4...]
where the time goes in v4:
time: 77.8 us; the launch traced here: 77.6 us
  Pallas kernels  76.9 us (99%)
    pallas_call x1, Pallas kernels, on_device(): pl.pallas_call(functools.partial(kernel, scale), out_shape=(pltpu.VMEM((4...  76.3 us

profile of v4, /device:TPU:1, one launch (start us, length us, event | category | flops | bytes accessed | tf_op | source)
XLA Modules:
  0.0 77.6 jit_solution(13202119354781859161)
XLA Ops:
  0.6 76.3 %shard_map.75 = (bf16[4,2,8,128]{3,2,1,0:T(8,128)(2,1)S(1)}, bf16[4,2,8,128]{3,2,1,0:T(8,128)(2,1)S(1)}, f32[128,256]{1,0:T(8,128)S(1)}) custom-call(bf16[4,2,8,128]{3,2,1,0:T(8,128)(2,1)} %x_hbm.1, bf16[27,4,256]{2,1,0:T(4,128)(2,1)} %bitcast.4, bf16[1,4]{1,0:T(2,128)(2,1)} %bitcast.5, bf16[4,2,8,128]{3,2,1,0:T(8,128)(2,1)} %go_hbm.1), custom_call_target="tpu_custom_call" | custom-call | tf_op jit(solution)/shard_map/pallas_call | solution.py:422
  76.9 0.7 shard_map.76

commit v5 on v4

--- a/solution.py
+++ b/solution.py
@@ -125,8 +125,8 @@
     def c_wait(self):
         landed(self.buf.at[:, :, :, :, 1 - self.k], self.rc)
 
-    def pair(self):
-        return jnp.concatenate([self.buf[p].reshape(2048, 128) for p in range(2)], axis=1)
+    def pair(self, *planes):
+        return jnp.concatenate([self.buf[p].reshape(2048, 128) for p in planes], axis=1)
 
 
 def band_weights(expanded, out, row_of, sign):
@@ -170,8 +170,8 @@
     x_hbm, w_hbm, bias_hbm, go_hbm,
     act_ref, ig_ref, out_ref,
     x_ref, w_ref, bias_ref, go_ref, load_sems,
-    xb, gb, rep, wide, spread, wa, wb, dm, rows, t1, t2, t3, t4, all_rows, dw, yb, zb, tot, po, pi, fo, fi, go_rim,
-    send_sems, xz, xn, xf, xc, gz, gn, gf, gc, s1, s2, s3, sy, sz, sg, sp, sf, so, ready,
+    xb, gb, rep, wide, spread, wa, wb, dm, rows, t1, t2, t3, t4, all_rows, dw, yb, zb, tot, fo, fi, go_rim,
+    send_sems, xz, xn, xf, xc, gz, gn, gf, gc, s1, s2, s3, sy, sz, sg, sf, so, ready,
 ):
     slab, chan = lax.axis_index("slab"), lax.axis_index("chan")
     y, zh = slab // NH, slab % NH
@@ -266,7 +266,7 @@
     copies.send(go_ref.at[:, 0], go_rim.at[1], so.at[1], before)
     gx_.c_wait()
 
-    own = jnp.dot(wa[...], gx_.pair(), preferred_element_type=F32)
+    own = jnp.dot(wa[...], gx_.pair(0, 1), preferred_element_type=F32)
 
     def part(value, i, l, o, p):
         base = ((i * 3 + l) * 4 + o) * 8
@@ -325,8 +325,8 @@
                 given = go_rim[n // 3, o]
             row.append(given.astype(F32) * (sig * (1.0 + pre * (1.0 - sig))))
         grads.append(jnp.concatenate(row, axis=0).astype(BF16))
-    gb[0, x, h, gx_.z4, k] = grads[1]
-    gb[1, x, h, gx_.z4, k] = grads[2]
+    for n in range(4):
+        gb[n, x, h, gx_.z4, k] = grads[n]
 
     gg_.z_send()
 
@@ -338,7 +338,7 @@
     lane = lax.broadcasted_iota(jnp.int32, (8, 2048), 1)
     sub = lax.broadcasted_iota(jnp.int32, (8, 2048), 0)
     tap = (lane - sub + 1) & 7
-    whole = lax.dot_general(rolled, gx_.pair(), NT, preferred_element_type=F32)
+    whole = lax.dot_general(rolled, gx_.pair(0, 1), NT, preferred_element_type=F32)
     sums = []
     for i in range(3):
         full = whole[96 * i : 96 * i + 96].reshape(12, 8, 2048)
@@ -354,8 +354,6 @@
     for m in range(1, NY):
         copies.send(dw.at[(y + m) % NY], yb.at[y], sy.at[y], at((y + m) % NY, zh))
 
-    gg_.z_mates()
-    gg_.z_mirror()
     yb[y] = dw[y]
     for m in range(1, NY):
         landed(yb.at[(y + m) % NY], sy.at[(y + m) % NY])
@@ -363,41 +361,39 @@
     for s in (1, NH - 1):
         copies.send(zb.at[zh], zb.at[zh], sz.at[zh], at(y, (zh + s) % NH))
 
+    gg_.z_mates()
+    gg_.z_mirror()
     gg_.x_near(None)
     gg_.near_to_core(h)
     gg_.z_far()
     gg_.x_near(gg_.z4)
+    for s in (1, NH - 1):
+        landed(zb.at[(zh + s) % NH], sz.at[(zh + s) % NH])
+    source, target = (zh + 3 + 2 * k) % NH, (zh + 1 + 2 * k) % NH
+    copies.send(zb.at[source], zb.at[source], sz.at[source], at(y, target))
     gg_.x_far(0)
     for mate in gg_.mates:
         gg_.x_near(mate)
     gg_.near_to_core(gg_.f)
-    for s in (1, NH - 1):
-        landed(zb.at[(zh + s) % NH], sz.at[(zh + s) % NH])
-    source, target = (zh + 3 + 2 * k) % NH, (zh + 1 + 2 * k) % NH
-    copies.send(zb.at[source], zb.at[source], sz.at[source], at(y, target))
     gg_.x_far(1)
     gg_.c_wait()
-    own2 = jnp.dot(wb[...], gg_.pair(), preferred_element_type=F32)
-    for c in range(4):
-        po[0, c] = turned_sum(lambda l: part(own2, 2, l, c, 1), -1).astype(BF16)
-        po[1, c] = turned_sum(lambda l: part(own2, 0, l, c, 0), -1).astype(BF16)
-    copies.send(po.at[0], pi.at[0], sp.at[0], after)
-    copies.send(po.at[1], pi.at[1], sp.at[1], before)
+    own2 = jnp.dot(wb[...], gg_.pair(1, 2), preferred_element_type=F32)
+    outer = jnp.concatenate([wb[0:96, :], wb[192:288, :]], axis=0)
+    rim = jnp.dot(outer, gg_.pair(0, 3), preferred_element_type=F32)
+    for p in range(2):
+        for c in range(4):
+            if p == 0:
+                terms = lambda l: part(own2, 0, l, c, 1) + part(own2, 1, l, c, 0) + part(rim, 1, l, c, 0)
+            else:
+                terms = lambda l: part(rim, 0, l, c, 1) + part(own2, 1, l, c, 1) + part(own2, 2, l, c, 0)
+            ig_ref[c, p] = turned_sum(terms, -1).astype(BF16)
     landed(zb.at[(zh + 2) % NH], sz.at[(zh + 2) % NH])
-    tot[y] = sum(zb[m].astype(F32) for m in range(NH)) * scale
+    tot[y] = sum(zb[m].astype(F32) for m in range(NH)).astype(BF16)
     for m in range(1, NY):
         copies.send(tot.at[y], tot.at[y], sg.at[y], at((y + m) % NY, zh))
-    for p in range(2):
-        landed(pi.at[p], sp.at[p])
-        for c in range(4):
-            if p == 0:
-                terms = lambda l: part(own2, 0, l, c, 1) + part(own2, 1, l, c, 0)
-            else:
-                terms = lambda l: part(own2, 1, l, c, 1) + part(own2, 2, l, c, 0)
-            ig_ref[c, p] = (turned_sum(terms, -1) + pi[p, c].astype(F32)).astype(BF16)
     for m in range(1, NY):
         landed(tot.at[(y + m) % NY], sg.at[(y + m) % NY])
-    out_ref[...] = tot[...].reshape(128, 256)
+    out_ref[...] = tot[...].astype(F32).reshape(128, 256) * scale
     copies.drain()
 
 
@@ -435,7 +431,7 @@
             pltpu.VMEM((4, 2, 8, 128), BF16),
             dma(4),
             pltpu.VMEM((2, NX, 2, 4, NK, 32, 128), BF16),
-            pltpu.VMEM((2, NX, 2, 4, NK, 32, 128), BF16),
+            pltpu.VMEM((4, NX, 2, 4, NK, 32, 128), BF16),
             pltpu.VMEM((256, 2048), BF16),
             pltpu.VMEM((128, 2048), F32),
             pltpu.VMEM((16, 128, 128), F32),
@@ -451,9 +447,7 @@
             pltpu.VMEM((4, 32, 256), BF16),
             pltpu.VMEM((4, 32, 256), BF16),
             pltpu.VMEM((4, 32, 256), BF16),
-            pltpu.VMEM((4, 32, 256), F32),
-            pltpu.VMEM((2, 4, 8, 128), BF16),
-            pltpu.VMEM((2, 4, 8, 128), BF16),
+            pltpu.VMEM((4, 32, 256), BF16),
             pltpu.VMEM((4, 4, 8, 128), BF16),
             pltpu.VMEM((4, 4, 8, 128), BF16),
             pltpu.VMEM((2, 4, 8, 128), BF16),
@@ -461,7 +455,7 @@
             dma(8), dma(5, 2), dma(2), pltpu.SemaphoreType.DMA,
             dma(8), dma(5, 2), dma(2), pltpu.SemaphoreType.DMA,
             dma(8), dma(4), pltpu.SemaphoreType.DMA,
-            dma(4), dma(4), dma(4), dma(2), dma(2), dma(2),
+            dma(4), dma(4), dma(4), dma(2), dma(2),
             pltpu.SemaphoreType.REGULAR,
         ],
         compiler_params=pltpu.CompilerParams(collective_id=0, has_side_effects=True),

time: 77.8 us -> 74.7 us (0.960)
  Pallas kernels: 76.9 us -> 73.9 us
    pallas_call x1, Pallas kernels: 76.3 us -> 73.2 us  [on_device(): pl.pallas_call(functools.partial(kernel, scale), out_shape=(pltpu.VMEM((4...]
where the time goes in v5:
time: 74.7 us; the launch traced here: 74.6 us
  Pallas kernels  73.9 us (99%)
    pallas_call x1, Pallas kernels, on_device(): pl.pallas_call(functools.partial(kernel, scale), out_shape=(pltpu.VMEM((4...  73.2 us

profile of v5, /device:TPU:1, one launch (start us, length us, event | category | flops | bytes accessed | tf_op | source)
XLA Modules:
  0.0 74.6 jit_solution(4757099115802488846)
XLA Ops:
  0.6 73.2 %shard_map.75 = (bf16[4,2,8,128]{3,2,1,0:T(8,128)(2,1)S(1)}, bf16[4,2,8,128]{3,2,1,0:T(8,128)(2,1)S(1)}, f32[128,256]{1,0:T(8,128)S(1)}) custom-call(bf16[4,2,8,128]{3,2,1,0:T(8,128)(2,1)} %x_hbm.1, bf16[27,4,256]{2,1,0:T(4,128)(2,1)} %bitcast.4, bf16[1,4]{1,0:T(2,128)(2,1)} %bitcast.5, bf16[4,2,8,128]{3,2,1,0:T(8,128)(2,1)} %go_hbm.1), custom_call_target="tpu_custom_call" | custom-call | tf_op jit(solution)/shard_map/pallas_call | solution.py:418
  73.9 0.7 shard_map.76

commit v6 on v5

--- a/solution.py
+++ b/solution.py
@@ -171,7 +171,7 @@
     act_ref, ig_ref, out_ref,
     x_ref, w_ref, bias_ref, go_ref, load_sems,
     xb, gb, rep, wide, spread, wa, wb, dm, rows, t1, t2, t3, t4, all_rows, dw, yb, zb, tot, fo, fi, go_rim,
-    send_sems, xz, xn, xf, xc, gz, gn, gf, gc, s1, s2, s3, sy, sz, sg, sf, so, ready,
+    send_sems, xz, xn, xf, xc, gz, gn, gf, gc, s1, s2, s3, sy, sz, sg, sf, so, pass_sem, ready,
 ):
     slab, chan = lax.axis_index("slab"), lax.axis_index("chan")
     y, zh = slab // NH, slab % NH
@@ -301,11 +301,6 @@
         landed(t3.at[xx_], s2.at[xx_])
     copies.send(t3, t4, s3, gx_.dev(x, z, 1 - k))
     landed(t4, s3)
-    all_rows[0:256, :] = t3[...].astype(F32).reshape(256, 128)
-    all_rows[256:512, :] = t4[...].astype(F32).reshape(256, 128)
-    turned_weights(all_rows, spread, wide, k)
-    band_weights(wide, wb, lambda t, j: t % 4 * 32 + t // 12 * 9 + j * 3 + t % 12 // 4, -1)
-
     landed(fi.at[0:2], sf.at[0])
     landed(fi.at[2:4], sf.at[1])
     for side in range(2):
@@ -354,6 +349,11 @@
     for m in range(1, NY):
         copies.send(dw.at[(y + m) % NY], yb.at[y], sy.at[y], at((y + m) % NY, zh))
 
+    all_rows[0:256, :] = t3[...].astype(F32).reshape(256, 128)
+    all_rows[256:512, :] = t4[...].astype(F32).reshape(256, 128)
+    turned_weights(all_rows, spread, wide, k)
+    band_weights(wide, wb, lambda t, j: t % 4 * 32 + t // 12 * 9 + j * 3 + t % 12 // 4, -1)
+
     yb[y] = dw[y]
     for m in range(1, NY):
         landed(yb.at[(y + m) % NY], sy.at[(y + m) % NY])
@@ -361,20 +361,44 @@
     for s in (1, NH - 1):
         copies.send(zb.at[zh], zb.at[zh], sz.at[zh], at(y, (zh + s) % NH))
 
+    source, target = (zh + 3 + 2 * k) % NH, (zh + 1 + 2 * k) % NH
+    passed = pltpu.make_async_remote_copy(
+        src_ref=zb.at[source],
+        dst_ref=zb.at[source],
+        send_sem=pass_sem,
+        recv_sem=sz.at[source],
+        device_id=at(y, target),
+        device_id_type=MESH,
+    )
+
+    def pass_on():
+        landed(zb.at[source], sz.at[source])
+        passed.start()
+
     gg_.z_mates()
     gg_.z_mirror()
     gg_.x_near(None)
     gg_.near_to_core(h)
+
+    @pl.when(zh % 2 == 1)
+    def _():
+        pass_on()
+
     gg_.z_far()
     gg_.x_near(gg_.z4)
-    for s in (1, NH - 1):
-        landed(zb.at[(zh + s) % NH], sz.at[(zh + s) % NH])
-    source, target = (zh + 3 + 2 * k) % NH, (zh + 1 + 2 * k) % NH
-    copies.send(zb.at[source], zb.at[source], sz.at[source], at(y, target))
+    @pl.when(zh % 2 == 0)
+    def _():
+        pass_on()
+
     gg_.x_far(0)
     for mate in gg_.mates:
         gg_.x_near(mate)
     gg_.near_to_core(gg_.f)
+    for m in (target, (zh + 2) % NH):
+        landed(zb.at[m], sz.at[m])
+    tot[y] = sum(zb[m].astype(F32) for m in range(NH)).astype(BF16)
+    for m in range(1, NY):
+        copies.send(tot.at[y], tot.at[y], sg.at[y], at((y + m) % NY, zh))
     gg_.x_far(1)
     gg_.c_wait()
     own2 = jnp.dot(wb[...], gg_.pair(1, 2), preferred_element_type=F32)
@@ -387,13 +411,10 @@
             else:
                 terms = lambda l: part(rim, 0, l, c, 1) + part(own2, 1, l, c, 1) + part(own2, 2, l, c, 0)
             ig_ref[c, p] = turned_sum(terms, -1).astype(BF16)
-    landed(zb.at[(zh + 2) % NH], sz.at[(zh + 2) % NH])
-    tot[y] = sum(zb[m].astype(F32) for m in range(NH)).astype(BF16)
-    for m in range(1, NY):
-        copies.send(tot.at[y], tot.at[y], sg.at[y], at((y + m) % NY, zh))
     for m in range(1, NY):
         landed(tot.at[(y + m) % NY], sg.at[(y + m) % NY])
     out_ref[...] = tot[...].astype(F32).reshape(128, 256) * scale
+    passed.wait_send()
     copies.drain()
 
 
@@ -455,7 +476,7 @@
             dma(8), dma(5, 2), dma(2), pltpu.SemaphoreType.DMA,
             dma(8), dma(5, 2), dma(2), pltpu.SemaphoreType.DMA,
             dma(8), dma(4), pltpu.SemaphoreType.DMA,
-            dma(4), dma(4), dma(4), dma(2), dma(2),
+            dma(4), dma(4), dma(4), dma(2), dma(2), pltpu.SemaphoreType.DMA,
             pltpu.SemaphoreType.REGULAR,
         ],
         compiler_params=pltpu.CompilerParams(collective_id=0, has_side_effects=True),

time: 74.7 us -> 73.1 us (0.979)
  Pallas kernels: 73.9 us -> 72 us
    pallas_call x1, Pallas kernels: 73.2 us -> 71.4 us  [on_device(): pl.pallas_call(functools.partial(kernel, scale), out_shape=(pltpu.VMEM((4...]
where the time goes in v6:
time: 73.1 us; the launch traced here: 72.7 us
  Pallas kernels  72 us (98%)
    pallas_call x1, Pallas kernels, on_device(): pl.pallas_call(functools.partial(kernel, scale), out_shape=(pltpu.VMEM((4...  71.4 us

profile of v6, /device:TPU:1, one launch (start us, length us, event | category | flops | bytes accessed | tf_op | source)
XLA Modules:
  0.0 72.7 jit_solution(16594126463479301166)
XLA Ops:
  0.6 71.4 %shard_map.75 = (bf16[4,2,8,128]{3,2,1,0:T(8,128)(2,1)S(1)}, bf16[4,2,8,128]{3,2,1,0:T(8,128)(2,1)S(1)}, f32[128,256]{1,0:T(8,128)S(1)}) custom-call(bf16[4,2,8,128]{3,2,1,0:T(8,128)(2,1)} %x_hbm.1, bf16[27,4,256]{2,1,0:T(4,128)(2,1)} %bitcast.4, bf16[1,4]{1,0:T(2,128)(2,1)} %bitcast.5, bf16[4,2,8,128]{3,2,1,0:T(8,128)(2,1)} %go_hbm.1), custom_call_target="tpu_custom_call" | custom-call | tf_op jit(solution)/shard_map/pallas_call | solution.py:439
  72.0 0.7 shard_map.76
